TPU v7x, 256 devices: a whole 4x4x8 slice. The times are simulated.
256 devices in a mesh: dp: 8 (over y, core), expert: 32 (over x, z).
Axes of the slice: x: 4, y: 4, z: 8, core: 2. Of those that a mesh axis runs over, the one named last changes fastest.
Arguments:
- cotangent: bfloat16 [32768, 2048], P(('dp', 'expert')), may hold values from -6 to 6
- gate_prob: bfloat16 [32768, 8], P(('dp', 'expert')), may hold values from 0.029907227 to 0.3984375
- routes: int32 [32768, 8], P(('dp', 'expert')), may hold values from 0 to 63, all different within a row; in each aligned block of 128 rows (0 to 127, 128 to 255, ...) at most 24 rows name the same one
- hidden: bfloat16 [8, 64, 32, 24, 768], P('dp', 'expert'), may hold values from -0.3984375 to 0.3984375
- down_weight: bfloat16 [64, 768, 2048], P('expert'), may hold values from -0.21875 to 0.21875
- sign_seed: int32 [2048], replicated, may hold values from 0 to 1
Outputs:
- grad_hidden: bfloat16 [8, 64, 32, 24, 768], P('dp', 'expert')
- grad_prob: float32 [32768, 8], P(('dp', 'expert'))
- grad_weight: float32 [2048, 64, 768], P('dp', 'expert')
Inputs may be any that keep to these rules, and one draw needn't show every extreme that they name: `routes`: each row names 8 different experts; in each device's block of 128 tokens no expert is named by more than 24 tokens, and in some block one expert is named by exactly 24.
All inputs are finite; a program needn't handle non-finite values.
Results may differ from a plain program's by a relative error of at most 0.015.
Values may be sent and summed in bfloat16 or wider, within the bound.
A program may use at most 128 MiB of HBM per device.

v0:
```python
import math

import jax
import jax.numpy as jnp
from jax import lax
from jax.sharding import PartitionSpec as P

BLOCK = 128


def hadamard(length):
    index_vec = jnp.arange(length, dtype=jnp.int32)
    anded = jnp.bitwise_and(index_vec[:, None], index_vec[None, :])
    parity = jnp.zeros((length, length), jnp.int32)
    for shift_by in range(max(length.bit_length() - 1, 1)):
        parity = parity + jnp.bitwise_and(jnp.right_shift(anded, shift_by), 1)
    return (1.0 - 2.0 * (parity % 2).astype(jnp.float32)) / math.sqrt(length)


def block_slots(routes, experts_all):
    hit_count = jnp.sum(
        (routes[:, :, None] == jnp.arange(experts_all, dtype=jnp.int32)).astype(jnp.int32),
        axis=1,
        dtype=jnp.int32,
    )
    before = jnp.cumsum(hit_count, axis=0, dtype=jnp.int32) - hit_count
    return jnp.take_along_axis(before, routes, axis=1)


def rotate(grad_term, sign_vec):
    row_total = grad_term.shape[0]
    shaped = grad_term.reshape(row_total // BLOCK, BLOCK, -1) * sign_vec.reshape(
        row_total // BLOCK, BLOCK, 1
    )
    turned = jnp.einsum("ij,bjx->bix", hadamard(BLOCK), shaped, precision=lax.Precision.HIGHEST)
    return turned.reshape(grad_term.shape)


def shards(cotangent, gate_prob, routes, hidden, down_weight, sign_seed):
    experts_here = down_weight.shape[0]
    sources = lax.axis_size("expert")
    capacity = hidden.shape[3]
    tok_rows, top_count = routes.shape
    features = cotangent.shape[1]
    hidden_units = hidden.shape[4]
    experts_all = experts_here * sources
    total_slots = experts_here * sources * capacity
    slot_rank = block_slots(routes, experts_all)
    slot_index = (routes % experts_here * sources + routes // experts_here) * capacity + slot_rank
    pair_count = tok_rows * top_count
    pair_table = jnp.full((total_slots,), pair_count, jnp.int32)
    pair_table = pair_table.at[slot_index.reshape(-1)].set(jnp.arange(pair_count, dtype=jnp.int32))
    send_grad = jnp.take(cotangent, pair_table // top_count, axis=0, mode="fill", fill_value=0)
    send_grad = send_grad.reshape(experts_here, sources, capacity, features)
    send_prob = jnp.take(gate_prob.reshape(-1), pair_table, axis=0, mode="fill", fill_value=0)
    send_prob = send_prob.reshape(experts_here, sources, capacity)
    recv_grad, recv_prob = (
        lax.all_to_all(send_grad, "expert", split_axis=1, concat_axis=1, tiled=True),
        lax.all_to_all(send_prob, "expert", split_axis=1, concat_axis=1, tiled=True),
    )
    slot_rows = sources * capacity
    grad_rows = recv_grad.reshape(experts_here, slot_rows, features)
    prob_rows = recv_prob.reshape(experts_here, slot_rows).astype(jnp.float32)[:, :, None]
    saved_rows = hidden.reshape(experts_here, slot_rows, hidden_units)
    back_grad = jnp.einsum(
        "erd,efd->erf", grad_rows, down_weight, preferred_element_type=jnp.float32
    )
    grad_hidden = (prob_rows * back_grad).astype(jnp.bfloat16).reshape(hidden.shape)
    slot_grad = jnp.sum(back_grad * saved_rows.astype(jnp.float32), axis=2).reshape(
        experts_here, sources, capacity
    )
    returned = lax.all_to_all(slot_grad, "expert", split_axis=1, concat_axis=1, tiled=True)
    grad_prob = returned.reshape(-1)[slot_index]
    weighted = (prob_rows * saved_rows.astype(jnp.float32)).astype(jnp.bfloat16)
    sign_vec = (2 * sign_seed - 1).astype(jnp.float32)
    product = jnp.einsum("erd,erf->def", grad_rows, weighted, preferred_element_type=jnp.float32)
    grad_weight = lax.psum_scatter(
        rotate(product, sign_vec).astype(jnp.bfloat16), "dp", scatter_dimension=0, tiled=True
    ).astype(jnp.float32)
    return (grad_hidden, grad_prob, grad_weight)


def solution(mesh):
    in_specs = (
        P(("dp", "expert"), None),
        P(("dp", "expert"), None),
        P(("dp", "expert"), None),
        P("dp", "expert", None, None, None),
        P("expert", None, None),
        P(),
    )
    out_specs = (
        P("dp", "expert", None, None, None),
        P(("dp", "expert"), None),
        P("dp", "expert", None),
    )
    return jax.shard_map(shards, mesh=mesh, in_specs=in_specs, out_specs=out_specs, check_vma=False)
```

profile of v0, /device:TPU:1, one launch (start us, length us, event | category | flops | bytes accessed | tf_op | source)
XLA Modules:
  0.0 330.7 jit_solution(11218860072794467696)
XLA Ops:
  7.2 0.0 copy-start
  7.2 0.8 convert_reduce_fusion
  8.0 0.7 bitcast_or_fusion
  8.7 0.1 copy.69
  8.8 0.2 reduce_window_sum.11
  8.9 0.1 copy.71
  9.0 0.1 reshape.136
  9.1 0.0 copy-start.3
  9.1 0.0 copy-start.5
  9.2 7.1 %gather_fusion.3 = s32[1024]{0:T(1024)S(1)} fusion(s32[128,64]{1,0:T(8,128)S(1)} %sub.26, s32[1024]{0:T(1024)S(1)} %reshape.136), kind=kCustom, calls=%fused_computation.3 | custom fusion | bytes 16384 | tf_op jit(solution)/shard_map/jit(take_along_axis)/gather | solution.py:27
  16.2 0.1 reshape.139
  16.4 0.0 copy-done.3
  16.4 0.1 copy.73
  16.5 0.1 reshape.103
  16.6 4.3 %scatter_custom_fusion = s32[1536]{0:T(1024)S(1)} fusion(s32[1024]{0:T(1024)S(1)} %bitcast.33, s32[1024]{0:T(1024)S(1)} %iota.14, s32[]{:T(128)} %constant.77.clone.1), kind=kCustom, calls=%fused_computation.71 | custom fusion | bytes 6148 | tf_op jit(solution)/shard_map/scatter | solution.py:52
  21.0 0.0 copy-done.5
  21.0 0.1 copy.74
  21.1 0.1 reshape.104
  21.2 9.5 %gather_fusion = bf16[1536]{0:T(1024)(128)(2,1)S(1)} fusion(bf16[1024]{0:T(1024)(128)(2,1)S(1)} %reshape.104, s32[2048]{0:T(1024)S(1)} %pad_clamp_fusion.1), kind=kCustom, calls=%fused_computation | custom fusion | bytes 12288 | tf_op jit(solution)/shard_map/jit(_take)/gather | solution.py:55
  30.7 0.1 select_n.72
  30.8 0.6 copy.75
  31.4 11.9 %all-to-all-start = ((bf16[2,32,24]{2,0,1:T(2,128)(2,1)}), bf16[2,32,24]{2,0,1:T(2,128)(2,1)S(1)}, u32[]{:S(2)}, u32[]{:S(2)}) async-start(bf16[2,32,24]{2,0,1:T(2,128)(2,1)} %copy.75), calls=%async_computation | async-start | bytes 32768 | tf_op jit(solution)/shard_map/all_to_all | solution.py:59
  43.3 0.1 broadcast_in_dim.42
  43.5 0.0 copy-done
  43.5 7.1 %gather_fusion.1 = bf16[1536,2048]{1,0:T(8,128)(2,1)} fusion(bf16[128,2048]{1,0:T(8,128)(2,1)S(1)} %copy-done, s32[2048]{0:T(1024)S(1)} %pad_clamp_fusion), kind=kCustom, calls=%fused_computation.1 | custom fusion | bytes 12589056 | tf_op jit(solution)/shard_map/jit(_take)/gather | solution.py:53
  50.6 6.5 %copy_select_fusion = bf16[2,32,24,2048]{3,2,0,1:T(8,128)(2,1)} fusion(bf16[2,32,24,2048]{3,2,1,0:T(8,128)(2,1)} %bitcast.29, pred[2,32,24]{2,0,1:T(4,128)(4,1)S(1)} %copy.78), kind=kLoop, calls=%fused_computation.7 | loop fusion | flops 3145728 | bytes 12584448 | tf_op jit(solution)/shard_map/jit(_take)/select_n | solution.py:53
  57.1 0.0 copy-start.4
  57.1 0.0 all-to-all-done
  57.1 9.5 %all-to-all-start.1 = ((bf16[2,32,24,2048]{3,2,0,1:T(8,128)(2,1)}), bf16[2,32,24,2048]{3,2,0,1:T(8,128)(2,1)}, u32[]{:S(2)}, u32[]{:S(2)}) async-start(bf16[2,32,24,2048]{3,2,0,1:T(8,128)(2,1)} %copy_select_fusion), calls=%async_computation.1 | async-start | bytes 12582912 | tf_op jit(solution)/shard_map/all_to_all | solution.py:58
  66.6 0.2 reduce-scatter.2.cloned.1.call-start
  66.8 0.0 copy-done.4
  66.8 0.1 copy.76
  66.9 0.1 copy.77
  67.0 0.1 reshape.110
  67.1 0.0 copy-start.6
  67.1 138.7 %all-to-all-done.1 = bf16[2,32,24,2048]{3,2,0,1:T(8,128)(2,1)} async-done(((bf16[2,32,24,2048]{3,2,0,1:T(8,128)(2,1)}), bf16[2,32,24,2048]{3,2,0,1:T(8,128)(2,1)}, u32[]{:S(2)}, u32[]{:S(2)}) %all-to-all-start.1) | async-done | bytes 6291488 | tf_op jit(solution)/shard_map/all_to_all | solution.py:58
  205.8 3.4 %copy.80 = bf16[2,32,24,2048]{3,2,1,0:T(8,128)(2,1)S(1)} copy(bf16[2,32,24,2048]{3,2,0,1:T(8,128)(2,1)} %all-to-all-done.1) | data formatting | bytes 12582912 | tf_op jit(solution)/shard_map/all_to_all | solution.py:58
  209.2 0.0 copy-start.2
  209.2 0.0 copy-done.6
  209.2 8.4 %fusion.4 = f32[2,768,2048]{2,1,0:T(8,128)} fusion(bf16[2,768,2048]{2,1,0:T(8,128)(2,1)S(1)} %bitcast.31, bf16[2,768,768]{2,1,0:T(8,128)(2,1)S(1)} %bitcast.34, f32[2,768]{1,0:T(2,128)S(1)} %reshape.110), kind=kOutput, calls=%fused_computation.15 | convolution fusion | flops 4835377152 | bytes 21239808 | tf_op jit(solution)/shard_map/erd,erf->def/dot_general | solution.py:76
  217.5 0.0 copy-done.2
  217.5 12.1 %copy.90 = f32[192,8,16,128]{3,2,1,0:T(8,128)} copy(f32[192,8,16,128]{3,1,2,0:T(8,128)} %bitcast.30) | data formatting | bytes 25165824
  229.7 16.4 %convert_bitcast_fusion = bf16[16,128,1536]{1,2,0:T(8,128)(2,1)S(1)} fusion(f32[16,128,1536]{1,0,2:T(8,128)} %bitcast.28, f32[16,128]{1,0:T(8,128)S(1)} %convert_bitcast_fusion.1), kind=kOutput, calls=%fused_computation.8 | convolution fusion | flops 4838719488 | bytes 18882560 | tf_op jit(solution)/shard_map/ij,bjx->bix/dot_general | solution.py:35
  246.1 18.5 %copy.86 = bf16[16,128,1536]{1,0,2:T(8,128)(2,1)} copy(bf16[16,128,1536]{1,2,0:T(8,128)(2,1)S(1)} %convert_bitcast_fusion) | data formatting | bytes 12582912 | tf_op jit(solution)/shard_map/convert_element_type | solution.py:78
  264.6 10.3 %convert_element_type.55 = bf16[2048,2,768]{0,2,1:T(8,128)(2,1)} reshape(bf16[16,128,1536]{1,0,2:T(8,128)(2,1)} %copy.86) | data formatting | bytes 12582912 | tf_op jit(solution)/shard_map/convert_element_type | solution.py:78
  274.8 0.0 reduce-scatter.2.cloned.1.call-update
  274.9 0.1 copy.83
  275.0 0.1 reshape.130
  275.0 10.4 %fusion.2 = (f32[2,768]{1,0:T(2,128)S(1)}, bf16[2,768,768]{2,1,0:T(8,128)(2,1)}) fusion(bf16[2,768,768]{2,1,0:T(8,128)(2,1)S(1)} %bitcast.35, f32[2,768]{1,0:T(2,128)S(1)} %reshape.110, bf16[2,768,2048]{2,1,0:T(8,128)(2,1)} %bitcast.32, bf16[2,768,2048]{2,1,0:T(8,128)(2,1)} %param.10), kind=kOutput, calls=%fused_computation.12 | convolution fusion | flops 4837734912 | bytes 17313792 | tf_op jit(solution)/shard_map/erd,efd->erf/dot_general | solution.py:65
  285.5 0.1 reshape.107
  285.6 0.6 copy.81
  286.2 9.4 %all-to-all-start.2 = ((f32[2,32,24]{2,0,1:T(2,128)}), f32[2,32,24]{2,0,1:T(2,128)S(1)}, u32[]{:S(2)}, u32[]{:S(2)}) async-start(f32[2,32,24]{2,0,1:T(2,128)} %copy.81), calls=%async_computation.2 | async-start | bytes 65536 | tf_op jit(solution)/shard_map/all_to_all | solution.py:72
  295.6 8.8 %all-to-all-done.2 = f32[2,32,24]{2,0,1:T(2,128)S(1)} async-done(((f32[2,32,24]{2,0,1:T(2,128)}), f32[2,32,24]{2,0,1:T(2,128)S(1)}, u32[]{:S(2)}, u32[]{:S(2)}) %all-to-all-start.2) | async-done | bytes 6176 | tf_op jit(solution)/shard_map/all_to_all | solution.py:72
  304.4 0.1 reshape.108
  304.5 0.0 copy-start.1
  304.5 6.2 %gather_fusion.2 = f32[1024]{0:T(1024)S(1)} fusion(f32[1536]{0:T(1024)S(1)} %reshape.108, s32[1024]{0:T(1024)S(1)} %broadcast_clamp_fusion), kind=kCustom, calls=%fused_computation.2 | custom fusion | bytes 12288 | tf_op jit(solution)/shard_map/gather | solution.py:73
  310.6 0.1 reshape.129
  310.7 0.7 copy.87
  311.4 9.3 %reduce-scatter.2.cloned.1.call-done = bf16[256,2,768]{0,2,1:T(8,128)(2,1)} async-done(((bf16[2048,2,768]{0,2,1:T(8,128)(2,1)}), bf16[256,2,768]{0,2,1:T(8,128)(2,1)}) %reduce-scatter.2.cloned.1.call-update) | async-done | bytes 786448 | tf_op jit(solution)/shard_map/reduce_scatter | solution.py:77
  320.6 3.2 copy.88
  323.8 0.0 copy-done.1
  (14 shorter events, 0.2 us)
Async XLA Ops:
  7.2 36.3 %copy-start = (bf16[128,2048]{1,0:T(8,128)(2,1)S(1)}, bf16[128,2048]{1,0:T(8,128)(2,1)}, u32[]{:S(2)}) copy-start(bf16[128,2048]{1,0:T(8,128)(2,1)} %param.6) | copy-start | bytes 1572868
  9.1 7.2 %copy-start.3 = (s32[128,8]{0,1:T(8,128)S(1)}, s32[128,8]{0,1:T(8,128)}, u32[]{:S(2)}) copy-start(s32[128,8]{0,1:T(8,128)} %param.8) | copy-start | bytes 12292
  9.1 11.8 %copy-start.5 = (bf16[128,8]{0,1:T(8,128)(2,1)S(1)}, bf16[128,8]{0,1:T(8,128)(2,1)}, u32[]{:S(2)}) copy-start(bf16[128,8]{0,1:T(8,128)(2,1)} %param.7) | copy-start | bytes 6148
  31.4 25.6 %all-to-all-start = ((bf16[2,32,24]{2,0,1:T(2,128)(2,1)}), bf16[2,32,24]{2,0,1:T(2,128)(2,1)S(1)}, u32[]{:S(2)}, u32[]{:S(2)}) async-start(bf16[2,32,24]{2,0,1:T(2,128)(2,1)} %copy.75), calls=%async_computation | async-start | bytes 32768 | tf_op jit(solution)/shard_map/all_to_all | solution.py:59
  57.1 9.7 %copy-start.4 = (s32[2048]{0:T(1024)S(1)}, s32[2048]{0:T(1024)}, u32[]{:S(2)}) copy-start(s32[2048]{0:T(1024)} %param.11) | copy-start | bytes 24580
  57.1 148.7 %all-to-all-start.1 = ((bf16[2,32,24,2048]{3,2,0,1:T(8,128)(2,1)}), bf16[2,32,24,2048]{3,2,0,1:T(8,128)(2,1)}, u32[]{:S(2)}, u32[]{:S(2)}) async-start(bf16[2,32,24,2048]{3,2,0,1:T(8,128)(2,1)} %copy_select_fusion), calls=%async_computation.1 | async-start | bytes 12582912 | tf_op jit(solution)/shard_map/all_to_all | solution.py:58
  66.6 254.1 %reduce-scatter.2.cloned.1.call-start = ((), (), s32[]{:S(2)}) async-start(), calls=%async_computation.4 | async-start | bytes 7077888 | tf_op jit(solution)/shard_map/reduce_scatter | solution.py:77
  67.1 142.1 %copy-start.6 = (bf16[1,2,32,24,768]{4,3,2,1,0:T(8,128)(2,1)S(1)}, bf16[1,2,32,24,768]{4,3,2,1,0:T(8,128)(2,1)}, u32[]{:S(2)}) copy-start(bf16[1,2,32,24,768]{4,3,2,1,0:T(8,128)(2,1)} %param.9) | copy-start | bytes 7077892
  209.2 8.4 %copy-start.2 = (bf16[2,32,24,2048]{3,2,1,0:T(8,128)(2,1)}, bf16[2,32,24,2048]{3,2,1,0:T(8,128)(2,1)S(1)}, u32[]{:S(2)}) copy-start(bf16[2,32,24,2048]{3,2,1,0:T(8,128)(2,1)S(1)} %copy.80) | copy-start | bytes 18874372
  286.2 18.1 %all-to-all-start.2 = ((f32[2,32,24]{2,0,1:T(2,128)}), f32[2,32,24]{2,0,1:T(2,128)S(1)}, u32[]{:S(2)}, u32[]{:S(2)}) async-start(f32[2,32,24]{2,0,1:T(2,128)} %copy.81), calls=%async_computation.2 | async-start | bytes 65536 | tf_op jit(solution)/shard_map/all_to_all | solution.py:72
  304.5 19.4 %copy-start.1 = (bf16[128,2048]{1,0:T(8,128)(2,1)S(1)}, bf16[128,2048]{1,0:T(8,128)(2,1)}, u32[]{:S(2)}) copy-start(bf16[128,2048]{1,0:T(8,128)(2,1)} %param.6) | copy-start | bytes 1572868
Sparse Core Ops, SparseCore 0:
  275.0 45.6 reduce-scatter.1
where the time goes:
time: 331 us
  waiting for transfers between devices  157 us (47%)
  local copies, waits for them, and re-layouts  85.3 us (26%)
  matrix products  35.2 us (11%)
  starting transfers between devices  30.9 us (9%)
  between operations  14.3 us (4%)
  other arithmetic  8.27 us (2%)
    all_to_all x1, waiting for transfers between devices, shards(): lax.all_to_all(send_grad, 'expert', split_axis=1, concat_axis=1, tiled=True)  139 us
    convert_element_type x2, local copies, waits for them, and re-layouts, shards(): rotate(product, sign_vec).astype(jnp.bfloat16)  28.8 us
    dot_general x1, matrix products, rotate(): jnp.einsum('ij,bjx->bix', hadamard(BLOCK), shaped, precision=lax.Precisio...  16.4 us
    unnamed x18, local copies, waits for them, and re-layouts  16.1 us
    all_to_all x1, starting transfers between devices, shards(): lax.all_to_all(send_prob, 'expert', split_axis=1, concat_axis=1, tiled=True)  11.9 us
    dot_general x1, matrix products, shards(): jnp.einsum('erd,efd->erf', grad_rows, down_weight, preferred_element_type...  10.4 us
    all_to_all x1, starting transfers between devices, shards(): lax.all_to_all(send_grad, 'expert', split_axis=1, concat_axis=1, tiled=True)  9.47 us
    gather x1, local copies, waits for them, and re-layouts, shards(): jnp.take(gate_prob.reshape(-1), pair_table, axis=0, mode='fill', fill_val...  9.46 us
  transfers between devices with their start and end apart: 4, of which 3 were waited for; matrix products, arithmetic and copies ran while one was open for 10% of the time, Pallas kernels for 0%

commit v1 on v0

v1 whole, which is shorter than its diff:
```python
import functools
import math

import jax
import jax.numpy as jnp
from jax import lax
from jax.experimental import pallas as pl
from jax.experimental.pallas import tpu as pltpu
from jax.sharding import PartitionSpec as P

MESH = pl.DeviceIdType.MESH
BLOCK = 128
NX, NY, NZ = 4, 4, 8
CH = 4
LANES = 128
CW = NY * LANES
MISS = -100.0
BF16, F32 = jnp.bfloat16, jnp.float32


def dot_nn(a, b):
    return lax.dot_general(a, b, (((1,), (0,)), ((), ())), preferred_element_type=F32)


def dot_nt(a, b):
    return lax.dot_general(a, b, (((1,), (1,)), ((), ())), preferred_element_type=F32)


def kernel(
    cot, hid_hbm, w_hbm, routes_t, gate_t, seed,
    gh_out, gp_out, gw_out,
    zbuf, sel, rg, xsend, relay_r, relay_l, wbuf, hid, weighted_t, acc,
    part, part_in, y_relay, y_fin, tab, gtab, s_tab, z_tab, d_tab, r_tab, r_mid, r_end,
    in_sem, w_sem, hid_sem,
    zs_full, zs_half, z_recv,
    xs_sem, x_recv, xrel_recv,
    tz_send, tz_recv, tx_send, tx_recv,
    p_send, p_recv, yr_send, yr_recv, yf_send, yf_recv,
    rx_send, rx_recv, rz_send, rz_recv,
):
    rows48 = 48
    dp = lax.axis_index("dp")
    ex = lax.axis_index("expert")
    y, core = dp // 2, lax.rem(dp, 2)
    x, z = ex // NZ, lax.rem(ex, NZ)
    up = lambda v, d, n: lax.rem(v + d, n)

    def x_dev(xx):
        return (dp, xx * NZ + z)

    def z_dev(zz):
        return (dp, x * NZ + zz)

    xr, xl = x_dev(up(x, 1, NX)), x_dev(up(x, NX - 1, NX))
    zr, zl = z_dev(up(z, 1, NZ)), z_dev(up(z, NZ - 1, NZ))
    yr, yl = (up(y, 1, NY) * 2 + core, ex), (up(y, NY - 1, NY) * 2 + core, ex)
    partner = (y * 2 + 1 - core, ex)

    def remote(src, dst, send, recv, dev):
        return pltpu.make_async_remote_copy(
            src_ref=src, dst_ref=dst, send_sem=send, recv_sem=recv,
            device_id=dev, device_id_type=MESH,
        )

    def wait_recv(dst, sem):
        remote(dst, dst, sem, sem, xr).wait_recv()

    def wait_send(src, sem):
        remote(src, src, sem, sem, xr).wait_send()

    for c in range(CH):
        for yy in range(NY):
            base = 512 * yy + 256 * (c % 2) + 128 * (c // 2)
            pltpu.make_async_copy(
                cot.at[:, pl.ds(base, LANES)],
                zbuf.at[c, z, :, pl.ds(LANES * yy, LANES)], in_sem.at[c],
            ).start()
    pltpu.make_async_copy(hid_hbm, hid, hid_sem).start()
    for c in range(CH):
        for yy in range(NY):
            base = 512 * yy + 256 * (c % 2) + 128 * (c // 2)
            pltpu.make_async_copy(
                w_hbm.at[:, :, pl.ds(base, LANES)],
                wbuf.at[c, :, :, pl.ds(LANES * yy, LANES)], w_sem.at[c],
            ).start()

    e_iota = lax.broadcasted_iota(jnp.int32, (64, LANES), 0)
    hit = jnp.zeros((64, LANES), F32)
    gate = jnp.zeros((64, LANES), F32)
    for k in range(8):
        eq = routes_t[k:k + 1, :] == e_iota
        hit = jnp.where(eq, 1.0, hit)
        gate = jnp.where(eq, gate_t[k:k + 1, :], gate)
    earlier = (
        lax.broadcasted_iota(jnp.int32, (LANES, LANES), 0)
        < lax.broadcasted_iota(jnp.int32, (LANES, LANES), 1)
    )
    rank = dot_nn(hit.astype(BF16), jnp.where(earlier, 1.0, 0.0).astype(BF16))
    tab[...] = jnp.where(hit > 0.5, rank, MISS)
    gtab[...] = gate
    for zz in range(NZ):
        for xx in range(NX):
            e = 16 * xx + 2 * zz
            s_tab[zz, xx, 0:2, :] = tab[e:e + 2, :]
            s_tab[zz, xx, 2:4, :] = gtab[e:e + 2, :]
            s_tab[zz, xx, 4:8, :] = jnp.zeros((4, LANES), F32)

    barrier = pltpu.get_barrier_semaphore()
    peers = [z_dev(up(z, d, NZ)) for d in range(1, NZ)]
    peers += [x_dev(up(x, d, NX)) for d in range(1, NX)]
    peers += [yr, yl, partner]
    for peer in peers:
        pl.semaphore_signal(barrier, inc=1, device_id=peer, device_id_type=MESH)
    pl.semaphore_wait(barrier, len(peers))

    for d in range(1, NZ):
        to = up(z, d, NZ)
        remote(s_tab.at[to], z_tab.at[z], tz_send.at[d], tz_recv.at[d], z_dev(to)).start()
    z_tab[z] = s_tab[z]

    def z_send(c, h):
        right, left = up(z, NZ - h, NZ), up(z, h, NZ)
        if h < 3:
            remote(zbuf.at[c, right], zbuf.at[c, right], zs_full.at[c, 0], z_recv.at[c, 0, h], zr).start()
            remote(zbuf.at[c, left], zbuf.at[c, left], zs_full.at[c, 1], z_recv.at[c, 1, h], zl).start()
        else:
            a, b = pl.ds(0, 64), pl.ds(64, 64)
            remote(zbuf.at[c, right, a], zbuf.at[c, right, a], zs_half.at[c, 0], z_recv.at[c, 0, h], zr).start()
            remote(zbuf.at[c, left, b], zbuf.at[c, left, b], zs_half.at[c, 1], z_recv.at[c, 1, h], zl).start()

    def z_wait(c, dist):
        from_left, from_right = up(z, NZ - dist, NZ), up(z, dist, NZ)
        if dist < 4:
            wait_recv(zbuf.at[c, from_left], z_recv.at[c, 0, dist - 1])
            wait_recv(zbuf.at[c, from_right], z_recv.at[c, 1, dist - 1])
        else:
            wait_recv(zbuf.at[c, from_left, pl.ds(0, 64)], z_recv.at[c, 0, dist - 1])
            wait_recv(zbuf.at[c, from_right, pl.ds(64, 64)], z_recv.at[c, 1, dist - 1])

    def in_wait(c):
        pltpu.make_async_copy(zbuf.at[c, z], zbuf.at[c, z], in_sem.at[c]).wait()

    in_wait(0)
    z_send(0, 0)

    for d in range(1, NZ):
        wait_recv(z_tab.at[up(z, NZ - d, NZ)], tz_recv.at[d])
    r_iota = lax.broadcasted_iota(jnp.int32, (rows48, LANES), 0).astype(F32)

    def one_hot_pair(even_row, odd_row):
        return even_row == r_iota, odd_row + 24.0 == r_iota

    def build_sel(m, _):
        for dx in range(NX):
            xx = up(x, dx, NX)
            for j in range(2):
                even, odd = one_hot_pair(
                    z_tab[2 * m, xx, j:j + 1, :], z_tab[2 * m + 1, xx, j:j + 1, :]
                )
                at = (dx * 2 + j) * rows48
                sel[m, at:at + rows48, 0:LANES] = jnp.where(even, 1.0, 0.0).astype(BF16)
                sel[m, at:at + rows48, LANES:2 * LANES] = jnp.where(odd, 1.0, 0.0).astype(BF16)
        return 0

    lax.fori_loop(0, 4, build_sel, 0)

    for d in range(1, NX):
        to = up(x, d, NX)
        remote(z_tab.at[:, to], d_tab.at[x], tx_send.at[d], tx_recv.at[d], x_dev(to)).start()
    d_tab[x] = z_tab[:, x]

    step_sign = 2 * lax.rem(z, 2) - 1
    pair_of = [up(z // 2, o, 4) for o in (0, 4 + step_sign, 4 - step_sign, 2)]

    def x_step(c, i):
        m = pair_of[i]
        tokens = zbuf[c, pl.ds(2 * m, 2)].reshape(2 * LANES, CW)
        rows = dot_nn(sel[m], tokens).astype(BF16)
        xsend[c, i] = rows[96:384].reshape(3, 2, rows48, CW)
        here = x * 4 + m
        remote(xsend.at[c, i, 1, 0], relay_r.at[c, i], xs_sem.at[c, 2], xrel_recv.at[c, i, 0], xr).start()
        remote(xsend.at[c, i, 1, 1], relay_l.at[c, i], xs_sem.at[c, 3], xrel_recv.at[c, i, 1], xl).start()
        remote(xsend.at[c, i, 0], rg.at[c, :, here], xs_sem.at[c, 0], x_recv.at[c, 0], xr).start()
        remote(xsend.at[c, i, 2], rg.at[c, :, here], xs_sem.at[c, 1], x_recv.at[c, 1], xl).start()
        rg[c, :, here] = rows[0:96].reshape(2, rows48, CW)

    def x_forward(c, i):
        m = pair_of[i]
        from_l, from_r = up(x, NX - 1, NX) * 4 + m, up(x, 1, NX) * 4 + m
        wait_recv(relay_r.at[c, i], xrel_recv.at[c, i, 0])
        remote(relay_r.at[c, i], rg.at[c, 0, from_l], xs_sem.at[c, 4], x_recv.at[c, 2], xr).start()
        wait_recv(relay_l.at[c, i], xrel_recv.at[c, i, 1])
        remote(relay_l.at[c, i], rg.at[c, 1, from_r], xs_sem.at[c, 5], x_recv.at[c, 3], xl).start()

    def x_wait(c):
        left, right, far = (pl.ds(up(x, d, NX) * 4, 4) for d in (3, 1, 2))
        wait_recv(rg.at[c, :, left], x_recv.at[c, 0])
        wait_recv(rg.at[c, :, right], x_recv.at[c, 1])
        wait_recv(rg.at[c, 0, far], x_recv.at[c, 2])
        wait_recv(rg.at[c, 1, far], x_recv.at[c, 3])

    def pair_rows(p, j, row):
        xs, zs = p // 4, 2 * lax.rem(p, 4)
        return d_tab[xs, zs, row + j:row + j + 1, :], d_tab[xs, zs + 1, row + j:row + j + 1, :]

    def slot_prob(p, j):
        even, odd = one_hot_pair(*pair_rows(p, j, 0))
        g_even, g_odd = pair_rows(p, j, 2)
        picked = jnp.where(even, g_even, 0.0) + jnp.where(odd, g_odd, 0.0)
        return jnp.sum(picked, axis=1, keepdims=True)

    def weigh():
        for d in range(1, NX):
            wait_recv(d_tab.at[up(x, NX - d, NX)], tx_recv.at[d])
        pltpu.make_async_copy(hid_hbm, hid, hid_sem).wait()

        def body(p, _):
            at = pl.ds(pl.multiple_of(p * rows48, 16), rows48)
            for j in range(2):
                rows = slot_prob(p, j) * hid[j, at, :].astype(F32)
                gh_out[j, at, :] = rows.astype(BF16)
            return 0

        lax.fori_loop(0, 16, body, 0)
        for j in range(2):
            for q in range(6):
                cols = slice(LANES * q, LANES * (q + 1))
                weighted_t[j, cols, :] = gh_out[j, :, cols].T

    def partial(c, j):
        for q in range(3):
            fs = slice(256 * q, 256 * (q + 1))
            got = dot_nn(weighted_t[j, fs, :], rg[c, j].reshape(768, CW)).astype(BF16)
            for yy in range(NY):
                part[c, yy, j, fs, :] = got[:, LANES * yy:LANES * (yy + 1)]

        @pl.when(lax.rem(c, 2) != core)
        def _():
            half = c // 2
            remote(part.at[c, :, j], part_in.at[half, :, j], p_send.at[half, j], p_recv.at[half, j], partner).start()

    def back(c, j):
        for q in range(3):
            rs = slice(256 * q, 256 * (q + 1))
            lhs = rg[c, j].reshape(768, CW)[rs]
            got = dot_nt(lhs, wbuf[c, j])

            acc[j, rs, :] += got

    def w_wait(c):
        pltpu.make_async_copy(wbuf.at[c], wbuf.at[c], w_sem.at[c]).wait()

    def pair_add(c, j):
        half = c // 2
        wait_recv(part_in.at[half, :, j], p_recv.at[half, j])

        def body(yy, _):
            total = part[c, yy, j].astype(F32) + part_in[half, yy, j].astype(F32)
            part[c, yy, j] = total.astype(BF16)
            return 0

        far = up(y, 2, NY)
        lax.fori_loop(0, NY, lambda o, t: body(up(far, o, NY), t), 0)
        if j == 0:
            remote(part.at[c, far, 0], y_relay.at[half, 0], yr_send.at[half, 0], yr_recv.at[half, 0], yr).start()
            near = up(y, 3, NY)
            remote(part.at[c, near, 0], y_fin.at[half, 1, 0], yf_send.at[half, 1, 0], yf_recv.at[half, 1, 0], yl).start()
        else:
            remote(part.at[c, far, 1], y_relay.at[half, 1], yr_send.at[half, 1], yr_recv.at[half, 1], yl).start()
            near = up(y, 1, NY)
            remote(part.at[c, near, 1], y_fin.at[half, 0, 1], yf_send.at[half, 0, 1], yf_recv.at[half, 0, 1], yr).start()

    def relay_add(c):
        half = c // 2
        for j, d, side, dev in ((0, 1, 0, yr), (1, 3, 1, yl)):
            near = up(y, d, NY)
            wait_recv(y_relay.at[half, j], yr_recv.at[half, j])
            total = part[c, near, j].astype(F32) + y_relay[half, j].astype(F32)
            part[c, near, j] = total.astype(BF16)
            remote(part.at[c, near, j], y_fin.at[half, side, j], yf_send.at[half, side, j], yf_recv.at[half, side, j], dev).start()

    def finish(c):
        half = c // 2
        i0 = lax.broadcasted_iota(jnp.int32, (BLOCK, BLOCK), 0)
        i1 = lax.broadcasted_iota(jnp.int32, (BLOCK, BLOCK), 1)
        bits = i0 & i1
        bits = bits ^ (bits >> 4)
        bits = bits ^ (bits >> 2)
        bits = bits ^ (bits >> 1)
        sign = (2 * seed[pl.ds(4 * y + 2 * core + half, 1), :] - 1).astype(F32)
        turn = (jnp.where((bits & 1) == 1, -1.0, 1.0) * sign).astype(BF16)
        out_rows = pl.ds(pl.multiple_of(half * BLOCK, BLOCK), BLOCK)
        for j in range(2):
            wait_recv(y_fin.at[half, 0, j], yf_recv.at[half, 0, j])
            wait_recv(y_fin.at[half, 1, j], yf_recv.at[half, 1, j])
            total = part[c, y, j].astype(F32) + y_fin[half, 0, j].astype(F32) + y_fin[half, 1, j].astype(F32)
            high = total.astype(BF16)
            low = (total - high.astype(F32)).astype(BF16)
            turned = (dot_nt(turn, high) + dot_nt(turn, low)) * (1.0 / math.sqrt(BLOCK))
            gw_out[out_rows, 768 * j:768 * (j + 1)] = turned

    acc[...] = jnp.zeros(acc.shape, F32)

    def chunk(c, _):
        owner = lambda v: lax.rem(v, 2) == core

        for i in range(4):
            @pl.when(c == 0)
            def _(i=i):
                z_wait(0, i + 1)
                if i < 3:
                    z_send(0, i + 1)

            if i == 3:
                @pl.when(c > 0)
                def _():
                    z_wait(c, 4)

            x_step(c, i)

            @pl.when(c + 1 < CH)
            def _(i=i):
                if i == 0:
                    in_wait(c + 1)
                else:
                    z_wait(c + 1, i)
                z_send(c + 1, i)

            if i == 0:
                @pl.when(c == 0)
                def _():
                    weigh()

                @pl.when(c > 0)
                def _():
                    x_forward(c - 1, 3)

                @pl.when((c > 1) & owner(c - 2))
                def _():
                    relay_add(c - 2)
            else:
                x_forward(c, i - 1)

            if i == 1:
                @pl.when(c > 0)
                def _():
                    x_wait(c - 1)
                    partial(c - 1, 0)

                @pl.when((c > 1) & owner(c - 2))
                def _():
                    finish(c - 2)
            if i == 2:
                @pl.when(c > 0)
                def _():
                    partial(c - 1, 1)
                    w_wait(c - 1)
                    back(c - 1, 0)
            if i == 3:
                @pl.when((c > 0) & owner(c - 1))
                def _():
                    pair_add(c - 1, 0)
                    pair_add(c - 1, 1)

                @pl.when(c > 0)
                def _():
                    back(c - 1, 1)
        return 0

    lax.fori_loop(0, CH, chunk, 0)

    last = CH - 1
    mine = core == last % 2
    x_forward(last, 3)

    @pl.when(core == (last - 1) % 2)
    def _():
        relay_add(last - 1)

    w_wait(last)
    x_wait(last)
    partial(last, 0)
    partial(last, 1)

    @pl.when(mine)
    def _():
        pair_add(last, 0)
        pair_add(last, 1)

    back(last, 0)

    @pl.when(core == (last - 1) % 2)
    def _():
        finish(last - 1)

    @pl.when(mine)
    def _():
        relay_add(last)

    back(last, 1)

    def outputs(p, _):
        at = pl.ds(pl.multiple_of(p * rows48, 16), rows48)
        xs, zs = p // 4, 2 * lax.rem(p, 4)
        for j in range(2):
            rows = acc[j, at, :]
            gh_out[j, at, :] = (slot_prob(p, j) * rows).astype(BF16)
            slot = jnp.sum(rows * hid[j, at, :].astype(F32), axis=1, keepdims=True)
            even, odd = one_hot_pair(*pair_rows(p, j, 0))
            r_tab[xs, zs, j:j + 1, :] = jnp.sum(jnp.where(even, slot, 0.0), axis=0, keepdims=True)
            r_tab[xs, zs + 1, j:j + 1, :] = jnp.sum(jnp.where(odd, slot, 0.0), axis=0, keepdims=True)
        return 0

    r_tab[...] = jnp.zeros(r_tab.shape, F32)
    lax.fori_loop(0, 16, outputs, 0)

    for d in range(1, NX):
        to = up(x, d, NX)
        remote(r_tab.at[to], r_mid.at[x], rx_send.at[d], rx_recv.at[d], x_dev(to)).start()
    r_mid[x] = r_tab[x]
    for d in range(1, NX):
        wait_recv(r_mid.at[up(x, NX - d, NX)], rx_recv.at[d])
    for d in range(1, NZ):
        to = up(z, d, NZ)
        remote(r_mid.at[:, to], r_end.at[z], rz_send.at[d], rz_recv.at[d], z_dev(to)).start()
    r_end[z] = r_mid[:, z]

    @pl.when(mine)
    def _():
        finish(last)

    for d in range(1, NZ):
        wait_recv(r_end.at[up(z, NZ - d, NZ)], rz_recv.at[d])
    grad_prob = jnp.zeros((8, LANES), F32)
    chosen = routes_t[...]
    for zz in range(NZ):
        for xx in range(NX):
            for j in range(2):
                e = 16 * xx + 2 * zz + j
                grad_prob = jnp.where(chosen == e, r_end[zz, xx, j:j + 1, :], grad_prob)
    gp_out[...] = grad_prob

    for d in range(1, NZ):
        wait_send(s_tab.at[0], tz_send.at[d])
        wait_send(r_mid.at[:, 0], rz_send.at[d])
    for d in range(1, NX):
        wait_send(z_tab.at[:, 0], tx_send.at[d])
        wait_send(r_tab.at[0], rx_send.at[d])
    for c in range(CH):
        for side in range(2):
            wait_send(zbuf.at[c, pl.ds(0, 3)], zs_full.at[c, side])
            wait_send(zbuf.at[c, 0, pl.ds(0, 64)], zs_half.at[c, side])
            wait_send(xsend.at[c, :, 2 * side], xs_sem.at[c, side])
            wait_send(xsend.at[c, :, 1, side], xs_sem.at[c, 2 + side])
            wait_send(relay_r.at[c], xs_sem.at[c, 4 + side])
        half = c // 2

        @pl.when(core == c % 2)
        def _(c=c, half=half):
            for j in range(2):
                wait_send(part.at[c, 0, 0], yr_send.at[half, j])
                for side in range(2):
                    wait_send(part.at[c, 0, 0], yf_send.at[half, side, j])

        @pl.when(core != c % 2)
        def _(c=c, half=half):
            for j in range(2):
                wait_send(part.at[c, :, j], p_send.at[half, j])


def shards(cotangent, gate_prob, routes, hidden, down_weight, sign_seed):
    tok, features = cotangent.shape
    _, pair, sources, cap, units = hidden.shape
    slots = sources * cap
    vm = pl.BlockSpec(memory_space=pltpu.VMEM)
    anyspec = pl.BlockSpec(memory_space=pl.ANY)
    dma = pltpu.SemaphoreType.DMA
    scratch = [
        pltpu.VMEM((CH, NZ, tok, CW), BF16),
        pltpu.VMEM((4, 384, 256), BF16),
        pltpu.VMEM((CH, 2, 16, 48, CW), BF16),
        pltpu.VMEM((CH, 4, 3, 2, 48, CW), BF16),
        pltpu.VMEM((CH, 4, 48, CW), BF16),
        pltpu.VMEM((CH, 4, 48, CW), BF16),
        pltpu.VMEM((CH, 2, units, CW), BF16),
        pltpu.VMEM((2, slots, units), BF16),
        pltpu.VMEM((2, units, slots), BF16),
        pltpu.VMEM((2, slots, units), F32),
        pltpu.VMEM((CH, NY, 2, units, LANES), BF16),
        pltpu.VMEM((2, NY, 2, units, LANES), BF16),
        pltpu.VMEM((2, 2, units, LANES), BF16),
        pltpu.VMEM((2, 2, 2, units, LANES), BF16),
        pltpu.VMEM((64, LANES), F32),
        pltpu.VMEM((64, LANES), F32),
        pltpu.VMEM((NZ, NX, 8, LANES), F32),
        pltpu.VMEM((NZ, NX, 8, LANES), F32),
        pltpu.VMEM((NX, NZ, 8, LANES), F32),
        pltpu.VMEM((NX, NZ, 8, LANES), F32),
        pltpu.VMEM((NX, NZ, 8, LANES), F32),
        pltpu.VMEM((NZ, NX, 8, LANES), F32),
        dma((CH,)), dma((CH,)), dma,
        dma((CH, 2)), dma((CH, 2)), dma((CH, 2, 4)),
        dma((CH, 6)), dma((CH, 4)), dma((CH, 4, 2)),
        dma((NZ,)), dma((NZ,)), dma((NX,)), dma((NX,)),
        dma((2, 2)), dma((2, 2)),
        dma((2, 2)), dma((2, 2)), dma((2, 2, 2)), dma((2, 2, 2)),
        dma((NX,)), dma((NX,)), dma((NZ,)), dma((NZ,)),
    ]
    grad_hidden, grad_prob, grad_weight = pl.pallas_call(
        kernel,
        out_shape=(
            jax.ShapeDtypeStruct((pair, slots, units), BF16),
            jax.ShapeDtypeStruct((8, tok), F32),
            jax.ShapeDtypeStruct((256, pair * units), F32),
        ),
        in_specs=[anyspec, anyspec, anyspec, vm, vm, vm],
        out_specs=(vm, vm, vm),
        scratch_shapes=scratch,
        compiler_params=pltpu.CompilerParams(
            collective_id=0, has_side_effects=True, vmem_limit_bytes=67043328
        ),
        name="routed_backward",
    )(
        cotangent,
        hidden.reshape(pair, slots, units),
        down_weight,
        routes.T,
        gate_prob.astype(F32).T,
        sign_seed.reshape(16, 128),
    )
    return (
        grad_hidden.reshape(hidden.shape),
        grad_prob.T,
        grad_weight.reshape(256, pair, units),
    )


def solution(mesh):
    in_specs = (
        P(("dp", "expert"), None),
        P(("dp", "expert"), None),
        P(("dp", "expert"), None),
        P("dp", "expert", None, None, None),
        P("expert", None, None),
        P(),
    )
    out_specs = (
        P("dp", "expert", None, None, None),
        P(("dp", "expert"), None),
        P("dp", "expert", None),
    )
    return jax.shard_map(shards, mesh=mesh, in_specs=in_specs, out_specs=out_specs, check_vma=False)
```

time: 331 us -> 125 us (0.38)
  waiting for transfers between devices: 157 us -> 0 us
  Pallas kernels: 0 us -> 118 us
  local copies, waits for them, and re-layouts: 85.3 us -> 5.25 us
  matrix products: 35.2 us -> 0 us
  starting transfers between devices: 30.9 us -> 0 us
  between operations: 14.3 us -> 0.65 us
  other arithmetic: 8.27 us -> 1.28 us
    all_to_all x3 -> x0, waiting for transfers between devices: 147 us -> none  [the longest x1 139 us: shards(): lax.all_to_all(send_grad, 'expert', split_axis=1, concat_axis=1, tiled=True)]
    pallas_call x0 -> x1, Pallas kernels: none -> 118 us  [shards(): pl.pallas_call(kernel, out_shape=(jax.ShapeDtypeStruct((pair, slots, unit...]
    dot_general x3 -> x0, matrix products: 35.2 us -> none  [the longest x1 16.4 us: rotate(): jnp.einsum('ij,bjx->bix', hadamard(BLOCK), shaped, precision=lax.Precisio...]
    all_to_all x3 -> x0, starting transfers between devices: 30.7 us -> none  [the longest x1 11.9 us: shards(): lax.all_to_all(send_prob, 'expert', split_axis=1, concat_axis=1, tiled=True)]
    gather x9 -> x0, local copies, waits for them, and re-layouts: 30.2 us -> none  [the longest x1 9.46 us: shards(): jnp.take(gate_prob.reshape(-1), pair_table, axis=0, mode='fill', fill_val...]
    convert_element_type x4 -> x0, local copies, waits for them, and re-layouts: 29 us -> none  [the longest x2 28.8 us: shards(): rotate(product, sign_vec).astype(jnp.bfloat16)]
    unnamed x18 -> x6, local copies, waits for them, and re-layouts: 16.1 us -> 2.01 us
    reduce_scatter x1 -> x0, waiting for transfers between devices: 9.27 us -> none  [shards(): lax.psum_scatter(rotate(product, sign_vec).astype(jnp.bfloat16), 'dp', sc...]
  transfers between devices with their start and end apart: 4 -> 0, of which waited for: 3 -> 0; matrix products, arithmetic and copies ran while one was open for 10% -> 0% of each run, Pallas kernels for 0% -> 0%
where the time goes in v1:
time: 125 us
  Pallas kernels  118 us (94%)
  local copies, waits for them, and re-layouts  5.25 us (4%)
  other arithmetic  1.28 us (1%)
    pallas_call x1, Pallas kernels, shards(): pl.pallas_call(kernel, out_shape=(jax.ShapeDtypeStruct((pair, slots, unit...  118 us
    reshape x1, local copies, waits for them, and re-layouts, shards(): grad_weight.reshape(256, pair, units)  3.25 us

profile of v1, /device:TPU:1, one launch (start us, length us, event | category | flops | bytes accessed | tf_op | source)
XLA Modules:
  0.0 124.9 jit_solution(18404038972284328560)
XLA Ops:
  0.6 1.3 %convert_bitcast_fusion.gate_t = f32[8,128]{1,0:T(8,128)} fusion(bf16[128,8]{0,1:T(8,128)(2,1)} %param.7), kind=kLoop, calls=%fused_computation | loop fusion | flops 1024 | bytes 6144 | tf_op jit(solution)/shard_map/transpose | solution.py:528
  1.9 117.7 %routed_backward.1 = (bf16[2,768,768]{2,1,0:T(8,128)(2,1)}, f32[8,128]{1,0:T(8,128)}, f32[256,1536]{1,0:T(8,128)}) custom-call(bf16[128,2048]{1,0:T(8,128)(2,1)} %cot.1, bf16[2,768,768]{2,1,0:T(8,128)(2,1)} %bitcast.7, bf16[2,768,2048]{2,1,0:T(8,128)(2,1)} %w_hbm.1, s32[8,128]{1,0:T(8,128)} %bitcast.10, f32[8,128]{1,0:T(8,128)} %convert_bitcast_fusion.gate_t, ...), custom_call_target="tpu_custom_call" | custom-call | tf_op jit(solution)/shard_map/routed_backward/pallas_call | solution.py:509
  119.6 0.0 copy-start
  119.6 3.2 %reshape.21 = f32[256,2,768]{2,1,0:T(2,128)} reshape(f32[256,1536]{1,0:T(8,128)} %get-tuple-element.8) | data formatting | bytes 3145728 | tf_op jit(solution)/shard_map/reshape | solution.py:534
  122.9 0.0 copy-done
  122.9 0.0 copy-start.1
  122.9 1.4 %copy.11 = bf16[1,2,32,24,768]{4,3,2,1,0:T(8,128)(2,1)} copy(bf16[1,2,32,24,768]{4,3,2,1,0:T(8,128)(2,1)S(1)} %bitcast.8) | data formatting | bytes 4718592
  124.3 0.0 copy-done.1
  124.3 0.6 copy.12
Async XLA Ops:
  119.6 3.3 %copy-start = (bf16[2,768,768]{2,1,0:T(8,128)(2,1)S(1)}, bf16[2,768,768]{2,1,0:T(8,128)(2,1)}, u32[]{:S(2)}) copy-start(bf16[2,768,768]{2,1,0:T(8,128)(2,1)} %get-tuple-element.6) | copy-start | bytes 7077892
  122.9 1.4 %copy-start.1 = (f32[8,128]{1,0:T(8,128)S(1)}, f32[8,128]{1,0:T(8,128)}, u32[]{:S(2)}) copy-start(f32[8,128]{1,0:T(8,128)} %get-tuple-element.7) | copy-start | bytes 12292

commit v2 on v0

v2 whole, which is shorter than its diff:
```python
import functools
import math

import jax
import jax.numpy as jnp
from jax import lax
from jax.experimental import pallas as pl
from jax.experimental.pallas import tpu as pltpu
from jax.sharding import PartitionSpec as P

MESH = pl.DeviceIdType.MESH
BLOCK = 128
NX, NY, NZ = 4, 4, 8
CH = 8
LANES = 128
CW = 2 * LANES
MISS = -100.0
BF16, F32 = jnp.bfloat16, jnp.float32


def dot_nn(a, b):
    return lax.dot_general(a, b, (((1,), (0,)), ((), ())), preferred_element_type=F32)


def dot_nt(a, b):
    return lax.dot_general(a, b, (((1,), (1,)), ((), ())), preferred_element_type=F32)


def kernel(
    cot, hid_hbm, w_hbm, routes_t, gate_t, seed,
    gh_out, gp_out, gw_out,
    zbuf, sel, rg, xsend, relay, wbuf, hid, weighted_t, acc, gh_buf, gw_buf,
    part, part_in, y_relay, y_fin,
    table, t_rows, x_rows, x_out, d_in, d_tab,
    r_tab, r_mid, r_out, r_end,
    load_sem, w_sem, hid_sem, out_sem,
    zs_sem, z_recv, tz_sem, tz_half, tz_recv,
    xs_sem, x_recv, xrel_recv, tx_sem, tx_recv,
    p_send, p_recv, yr_send, yr_recv, yf_send, yf_recv,
    rx_send, rx_recv, rz_send, rz_recv,
):
    rows48 = 48
    dp = lax.axis_index("dp")
    ex = lax.axis_index("expert")
    y, core = dp // 2, lax.rem(dp, 2)
    x, z = ex // NZ, lax.rem(ex, NZ)
    up = lambda v, d, n: lax.rem(v + d, n)

    def x_dev(xx):
        return (dp, xx * NZ + z)

    def z_dev(zz):
        return (dp, x * NZ + zz)

    xr, xl = x_dev(up(x, 1, NX)), x_dev(up(x, NX - 1, NX))
    zr, zl = z_dev(up(z, 1, NZ)), z_dev(up(z, NZ - 1, NZ))
    yr, yl = (up(y, 1, NY) * 2 + core, ex), (up(y, NY - 1, NY) * 2 + core, ex)
    partner = (y * 2 + 1 - core, ex)

    def remote(src, dst, send, recv, dev):
        return pltpu.make_async_remote_copy(
            src_ref=src, dst_ref=dst, send_sem=send, recv_sem=recv,
            device_id=dev, device_id_type=MESH,
        )

    def wait_recv(dst, sem):
        remote(dst, dst, sem, sem, xr).wait_recv()

    def wait_send(src, sem):
        remote(src, src, sem, sem, xr).wait_send()

    barrier = pltpu.get_barrier_semaphore()
    peers = [zr, zl, yr, yl, partner]
    peers += [x_dev(up(x, d, NX)) for d in range(1, NX)]
    for peer in peers:
        pl.semaphore_signal(barrier, inc=1, device_id=peer, device_id_type=MESH)

    def base_of(c, k):
        return 512 * ((c + 2 * k) % NY) + 256 * k + LANES * (c // NY)

    for c in range(CH):
        for k in range(2):
            pltpu.make_async_copy(
                cot.at[:, pl.ds(base_of(c, k), LANES)],
                zbuf.at[c, z, :, pl.ds(LANES * k, LANES)], load_sem,
            ).start()
    pltpu.make_async_copy(hid_hbm, hid, hid_sem).start()
    for c in range(CH):
        for k in range(2):
            pltpu.make_async_copy(
                w_hbm.at[:, :, pl.ds(base_of(c, k), LANES)],
                wbuf.at[c, :, :, pl.ds(LANES * k, LANES)], w_sem,
            ).start()

    e_iota = lax.broadcasted_iota(jnp.int32, (64, LANES), 0)
    gates = gate_t[...].astype(F32)
    hit = jnp.zeros((64, LANES), F32)
    gate = jnp.zeros((64, LANES), F32)
    for k in range(8):
        eq = routes_t[k:k + 1, :] == e_iota
        hit = jnp.where(eq, 1.0, hit)
        gate = jnp.where(eq, gates[k:k + 1, :], gate)
    earlier = (
        lax.broadcasted_iota(jnp.int32, (LANES, LANES), 0)
        < lax.broadcasted_iota(jnp.int32, (LANES, LANES), 1)
    )
    rank = dot_nn(hit.astype(BF16), jnp.where(earlier, 1.0, 0.0).astype(BF16))
    table[z, 0:64, :] = jnp.where(hit > 0.5, rank, MISS).astype(BF16)
    table[z, 64:128, :] = gate.astype(BF16)
    pltpu.make_async_copy(zbuf.at[:, z], zbuf.at[:, z], load_sem).wait()
    pl.semaphore_wait(barrier, len(peers))

    lower, upper = pl.ds(0, 64), pl.ds(64, 64)

    def z_send(c, h):
        right, left = up(z, NZ - h, NZ), up(z, h, NZ)
        if h < 3:
            remote(zbuf.at[c, right], zbuf.at[c, right], zs_sem.at[0], z_recv.at[c, h], zr).start()
            remote(zbuf.at[c, left], zbuf.at[c, left], zs_sem.at[1], z_recv.at[c, h], zl).start()
        else:
            remote(zbuf.at[c, right, lower], zbuf.at[c, right, lower], zs_sem.at[0], z_recv.at[c, h], zr).start()
            remote(zbuf.at[c, left, upper], zbuf.at[c, left, upper], zs_sem.at[1], z_recv.at[c, h], zl).start()

    def z_wait(c, dist):
        wait_recv(zbuf.at[c, pl.ds(0, 2 if dist < 4 else 1)], z_recv.at[c, dist - 1])

    def z_relay(c, h):
        if h > 0:
            z_wait(c, h)
        z_send(c, h)

    def table_send(h):
        right, left = up(z, NZ - h, NZ), up(z, h, NZ)
        if h < 3:
            remote(table.at[right], table.at[right], tz_sem.at[0], tz_recv.at[h], zr).start()
            remote(table.at[left], table.at[left], tz_sem.at[1], tz_recv.at[h], zl).start()
        else:
            remote(table.at[right, lower], table.at[right, lower], tz_half.at[0], tz_recv.at[h], zr).start()
            remote(table.at[left, upper], table.at[left, upper], tz_half.at[1], tz_recv.at[h], zl).start()

    def table_rows(zs):
        block = table[zs].astype(F32)
        t_rows[zs] = block

    def table_wait(dist):
        wait_recv(table.at[pl.ds(0, 2 if dist < 4 else 1)], tz_recv.at[dist - 1])
        if dist < 4:
            table_send(dist)
            table_rows(up(z, NZ - dist, NZ))
        table_rows(up(z, dist, NZ))

    table_send(0)
    z_send(0, 0)
    z_send(1, 0)
    table_rows(z)

    r_iota = lax.broadcasted_iota(jnp.int32, (rows48, LANES), 0).astype(F32)

    def one_hot_pair(even_row, odd_row):
        return even_row == r_iota, odd_row + 24.0 == r_iota

    def build_sel(m):
        for dx in range(NX):
            xx = up(x, dx, NX)
            for j in range(2):
                row = pl.ds(16 * xx + 2 * z + j, 1)
                even, odd = one_hot_pair(t_rows[2 * m, row, :], t_rows[2 * m + 1, row, :])
                at = (dx * 2 + j) * rows48
                sel[m, at:at + rows48, 0:LANES] = jnp.where(even, 1.0, 0.0).astype(BF16)
                sel[m, at:at + rows48, LANES:2 * LANES] = jnp.where(odd, 1.0, 0.0).astype(BF16)

    def x_tables():
        for xx in range(NX):
            row = 16 * xx + 2 * z
            for zs in range(NZ):
                for j in range(2):
                    at = 2 * zs + j
                    x_rows[xx, at:at + 1, :] = t_rows[zs, pl.ds(row + j, 1), :]
                    x_rows[xx, 16 + at:17 + at, :] = t_rows[zs, pl.ds(64 + row + j, 1), :]
            x_out[xx] = x_rows[xx].astype(BF16)
        for d in range(1, NX):
            to = up(x, d, NX)
            remote(x_out.at[to], d_in.at[x], tx_sem, tx_recv, x_dev(to)).start()
        d_in[x] = x_out[x]

    step_sign = 2 * lax.rem(z, 2) - 1

    def pair_of(i):
        turn = jnp.where(i == 0, 0, jnp.where(i == 1, 4 + step_sign, jnp.where(i == 2, 4 - step_sign, 2)))
        return lax.rem(z // 2 + turn, 4)

    def step_of(s, t):
        if t < 0:
            s, t = s - 1, t + 8
        tail = s == 3
        return (
            jnp.where(tail, 6 + t // 4, 2 * s + t % 2),
            jnp.where(tail, t % 4, t // 2),
        )

    def x_step(c, i):
        m = pair_of(i)
        tokens = zbuf[c, pl.ds(2 * m, 2)].reshape(2 * LANES, CW)
        rows = dot_nn(sel[m], tokens).astype(BF16)
        xsend[c, i] = rows[96:384].reshape(3, 2, rows48, CW)
        here = x * 4 + m
        remote(xsend.at[c, i, 1, 0], relay.at[c, i, 0], xs_sem.at[2], xrel_recv.at[c, i], xr).start()
        remote(xsend.at[c, i, 1, 1], relay.at[c, i, 1], xs_sem.at[3], xrel_recv.at[c, i], xl).start()
        remote(xsend.at[c, i, 0], rg.at[c, :, here], xs_sem.at[0], x_recv.at[c], xr).start()
        remote(xsend.at[c, i, 2], rg.at[c, :, here], xs_sem.at[1], x_recv.at[c], xl).start()
        rg[c, :, here] = rows[0:96].reshape(2, rows48, CW)

    def x_forward(c, i):
        m = pair_of(i)
        from_l, from_r = up(x, NX - 1, NX) * 4 + m, up(x, 1, NX) * 4 + m
        wait_recv(relay.at[c, i], xrel_recv.at[c, i])
        remote(relay.at[c, i, 0], rg.at[c, 0, from_l], xs_sem.at[4], x_recv.at[c], xr).start()
        remote(relay.at[c, i, 1], rg.at[c, 1, from_r], xs_sem.at[5], x_recv.at[c], xl).start()

    def x_wait(c):
        wait_recv(rg.at[c, :, pl.ds(0, 12)], x_recv.at[c])

    def pair_rows(p, j, row):
        xs, at = p // 4, 4 * lax.rem(p, 4) + j + row
        return d_tab[xs, pl.ds(at, 1), :], d_tab[xs, pl.ds(at + 2, 1), :]

    def slot_prob(p, j):
        even, odd = one_hot_pair(*pair_rows(p, j, 0))
        g_even, g_odd = pair_rows(p, j, 16)
        picked = jnp.where(even, g_even, 0.0) + jnp.where(odd, g_odd, 0.0)
        return jnp.sum(picked, axis=1, keepdims=True)

    def weigh():
        wait_recv(d_in.at[pl.ds(0, 3)], tx_recv)
        d_tab[...] = d_in[...].astype(F32)
        pltpu.make_async_copy(hid_hbm, hid, hid_sem).wait()

        def body(p, _):
            at = pl.ds(pl.multiple_of(p * rows48, 16), rows48)
            for j in range(2):
                rows = slot_prob(p, j) * hid[j, at, :].astype(F32)
                gh_buf[j, at, :] = rows.astype(BF16)
            return 0

        lax.fori_loop(0, 16, body, 0)
        for j in range(2):
            for q in range(6):
                cols = slice(LANES * q, LANES * (q + 1))
                weighted_t[j, cols, :] = gh_buf[j, :, cols].T

    def partial(c):
        for j in range(2):
            for q in range(3):
                fs = slice(256 * q, 256 * (q + 1))
                got = dot_nn(weighted_t[j, fs, :], rg[c, j].reshape(768, CW)).astype(BF16)
                for k in range(2):
                    part[c, k, j, fs, :] = got[:, LANES * k:LANES * (k + 1)]
            remote(part.at[c, 1 - core, j], part_in.at[c, j], p_send, p_recv.at[c], partner).start()

    def back(c):
        for j in range(2):
            for q in range(3):
                rs = slice(256 * q, 256 * (q + 1))
                acc[j, rs, :] += dot_nt(rg[c, j].reshape(768, CW)[rs], wbuf[c, j])

    def role(c):
        return up(y + NY, NY - lax.rem(c + 2 * core, NY), NY)

    def pair_add(c):
        half, at = c // NY, role(c)
        wait_recv(part_in.at[c], p_recv.at[c])
        for j in range(2):
            total = part[c, core, j].astype(F32) + part_in[c, j].astype(F32)
            part[c, core, j] = total.astype(BF16)
        mine = part.at[c, core]

        @pl.when(at == 2)
        def _():
            remote(mine.at[0], y_relay.at[half, 0], yr_send, yr_recv.at[half, 0], yr).start()
            remote(mine.at[1], y_relay.at[half, 1], yr_send, yr_recv.at[half, 1], yl).start()

        @pl.when(at == 3)
        def _():
            remote(mine.at[1], y_fin.at[half, 0, 1], yf_send, yf_recv.at[half], yr).start()

        @pl.when(at == 1)
        def _():
            remote(mine.at[0], y_fin.at[half, 1, 0], yf_send, yf_recv.at[half], yl).start()

    def relay_add(c):
        half, at = c // NY, role(c)
        for j, place, side, dev in ((0, 3, 0, yr), (1, 1, 1, yl)):
            @pl.when(at == place)
            def _(j=j, side=side, dev=dev):
                wait_recv(y_relay.at[half, j], yr_recv.at[half, j])
                total = part[c, core, j].astype(F32) + y_relay[half, j].astype(F32)
                part[c, core, j] = total.astype(BF16)
                remote(part.at[c, core, j], y_fin.at[half, side, j], yf_send, yf_recv.at[half], dev).start()

    def finish(c):
        half = c // NY

        @pl.when(role(c) == 0)
        def _():
            i0 = lax.broadcasted_iota(jnp.int32, (BLOCK, BLOCK), 0)
            i1 = lax.broadcasted_iota(jnp.int32, (BLOCK, BLOCK), 1)
            bits = i0 & i1
            bits = bits ^ (bits >> 4)
            bits = bits ^ (bits >> 2)
            bits = bits ^ (bits >> 1)
            sign = (2 * seed[pl.ds(4 * y + 2 * core + half, 1), :] - 1).astype(F32)
            turn = (jnp.where((bits & 1) == 1, -1.0, 1.0) * sign).astype(BF16)
            out_rows = pl.ds(pl.multiple_of(half * BLOCK, BLOCK), BLOCK)
            wait_recv(y_fin.at[half], yf_recv.at[half])
            for j in range(2):
                total = part[c, core, j].astype(F32) + y_fin[half, 0, j].astype(F32) + y_fin[half, 1, j].astype(F32)
                high = total.astype(BF16)
                low = (total - high.astype(F32)).astype(BF16)
                turned = (dot_nt(turn, high) + dot_nt(turn, low)) * (1.0 / math.sqrt(BLOCK))
                gw_buf[out_rows, 768 * j:768 * (j + 1)] = turned
            pltpu.make_async_copy(gw_buf.at[out_rows], gw_out.at[out_rows], out_sem.at[half]).start()

    acc[...] = jnp.zeros(acc.shape, F32)

    def double(s, _):
        first, more = s == 0, s > 0
        for t in range(8):
            q, h = t % 2, t // 2

            @pl.when(first)
            def _(q=q, h=h):
                z_wait(q, h + 1)
                if h < 3:
                    z_send(q, h + 1)
                if q == 0:
                    table_wait(h + 1)
                    build_sel(pair_of(h))

            if t in (0, 1, 2):
                @pl.when(more)
                def _(t=t):
                    if t == 0:
                        z_relay(2 * s + 1, 2)
                    else:
                        z_relay(2 * s + t - 1, 3)
            else:
                @pl.when(s < 3)
                def _(t=t):
                    z_relay(2 * s + 2 + (t - 3) % 2, (t - 3) // 2)

            c, i = step_of(s, t)
            if t in (3, 6, 7):
                @pl.when(more & (i == 3))
                def _(c=c):
                    z_wait(c, 4)
            x_step(c, i)
            fc, fi = step_of(s, t - 3)
            if t < 3:
                @pl.when(more)
                def _(fc=fc, fi=fi):
                    x_forward(fc, fi)
            else:
                x_forward(fc, fi)

            a, b = 2 * s - 2, 2 * s - 1
            if t == 2:
                @pl.when(s == 1)
                def _():
                    weigh()
            if t in (1, 2):
                @pl.when(s > 1)
                def _(t=t):
                    finish(2 * s - 5 + t)
            if t == 3:
                @pl.when(more)
                def _():
                    x_wait(a)
                    partial(a)
            if t == 4:
                @pl.when(more)
                def _():
                    x_wait(b)
                    partial(b)
            if t == 5:
                @pl.when(s == 1)
                def _():
                    pltpu.make_async_copy(wbuf, wbuf, w_sem).wait()

                @pl.when(more)
                def _():
                    back(a)
                    pair_add(a)
            if t == 6:
                @pl.when(more)
                def _():
                    back(b)
                    pair_add(b)
            if t == 7:
                @pl.when(first)
                def _():
                    x_tables()

                @pl.when(more)
                def _():
                    relay_add(a)
                    relay_add(b)
        return 0

    lax.fori_loop(0, CH // 2, double, 0)

    x_forward(7, 1)
    x_forward(7, 2)
    x_wait(6)
    partial(6)
    x_forward(7, 3)
    back(6)
    pair_add(6)
    finish(4)
    finish(5)
    x_wait(7)
    partial(7)
    back(7)
    pair_add(7)
    relay_add(6)

    def outputs(p, _):
        at = pl.ds(pl.multiple_of(p * rows48, 16), rows48)
        xs, row = p // 4, 4 * lax.rem(p, 4)
        for j in range(2):
            rows = acc[j, at, :]
            gh_buf[j, at, :] = (slot_prob(p, j) * rows).astype(BF16)
            slot = jnp.sum(rows * hid[j, at, :].astype(F32), axis=1, keepdims=True)
            even, odd = one_hot_pair(*pair_rows(p, j, 0))
            r_tab[xs, pl.ds(row + j, 1), :] = jnp.sum(jnp.where(even, slot, 0.0), axis=0, keepdims=True)
            r_tab[xs, pl.ds(row + 2 + j, 1), :] = jnp.sum(jnp.where(odd, slot, 0.0), axis=0, keepdims=True)
        return 0

    lax.fori_loop(0, 8, outputs, 0)
    relay_add(7)
    lax.fori_loop(8, 16, outputs, 0)

    for d in range(1, NX):
        to = up(x, d, NX)
        remote(r_tab.at[to], r_mid.at[x], rx_send, rx_recv, x_dev(to)).start()
    r_mid[x] = r_tab[x]
    pltpu.make_async_copy(gh_buf, gh_out, hid_sem).start()
    finish(6)
    wait_recv(r_mid.at[pl.ds(0, 3)], rx_recv)
    for zs in range(NZ):
        for xx in range(NX):
            r_out[zs, 2 * xx:2 * xx + 2, :] = r_mid[xx, 2 * zs:2 * zs + 2, :]
    for d in range(1, NZ):
        to = up(z, d, NZ)
        remote(r_out.at[to], r_end.at[z], rz_send, rz_recv, z_dev(to)).start()
    r_end[z] = r_out[z]
    finish(7)
    wait_recv(r_end.at[pl.ds(0, 7)], rz_recv)
    grad_prob = jnp.zeros((8, LANES), F32)
    chosen = routes_t[...]
    for zz in range(NZ):
        for xx in range(NX):
            for j in range(2):
                e = 16 * xx + 2 * zz + j
                row = 2 * xx + j
                grad_prob = jnp.where(chosen == e, r_end[zz, row:row + 1, :], grad_prob)
    gp_out[...] = grad_prob

    wait_send(zbuf.at[pl.ds(0, 4), pl.ds(0, 7)], zs_sem.at[0])
    wait_send(zbuf.at[pl.ds(0, 4), pl.ds(0, 7)], zs_sem.at[1])
    for side in range(2):
        wait_send(table.at[pl.ds(0, 3)], tz_sem.at[side])
        wait_send(table.at[0, lower], tz_half.at[side])
        wait_send(xsend.at[:, :, 2 * side], xs_sem.at[side])
        wait_send(xsend.at[:, :, 1, side], xs_sem.at[2 + side])
        wait_send(relay.at[:, :, side], xs_sem.at[4 + side])
    wait_send(x_out.at[pl.ds(0, 3)], tx_sem)
    wait_send(r_tab.at[pl.ds(0, 3)], rx_send)
    wait_send(r_out.at[pl.ds(0, 7)], rz_send)
    wait_send(part.at[:, 0], p_send)
    wait_send(part.at[pl.ds(0, 2), 0], yr_send)
    wait_send(part.at[pl.ds(0, 4), 0], yf_send)
    pltpu.make_async_copy(gh_buf, gh_out, hid_sem).wait()
    for half in range(2):
        out_rows = pl.ds(BLOCK * half, BLOCK)
        pltpu.make_async_copy(gw_buf.at[out_rows], gw_out.at[out_rows], out_sem.at[half]).wait()


def shards(cotangent, gate_prob, routes, hidden, down_weight, sign_seed):
    tok, features = cotangent.shape
    _, pair, sources, cap, units = hidden.shape
    slots = sources * cap
    vm = pl.BlockSpec(memory_space=pltpu.VMEM)
    anyspec = pl.BlockSpec(memory_space=pl.ANY)
    dma = pltpu.SemaphoreType.DMA
    scratch = [
        pltpu.VMEM((CH, NZ, tok, CW), BF16),
        pltpu.VMEM((4, 384, 256), BF16),
        pltpu.VMEM((CH, 2, 16, 48, CW), BF16),
        pltpu.VMEM((CH, 4, 3, 2, 48, CW), BF16),
        pltpu.VMEM((CH, 4, 2, 48, CW), BF16),
        pltpu.VMEM((CH, 2, units, CW), BF16),
        pltpu.VMEM((2, slots, units), BF16),
        pltpu.VMEM((2, units, slots), BF16),
        pltpu.VMEM((2, slots, units), F32),
        pltpu.VMEM((2, slots, units), BF16),
        pltpu.VMEM((256, pair * units), F32),
        pltpu.VMEM((CH, 2, 2, units, LANES), BF16),
        pltpu.VMEM((CH, 2, units, LANES), BF16),
        pltpu.VMEM((2, 2, units, LANES), BF16),
        pltpu.VMEM((2, 2, 2, units, LANES), BF16),
        pltpu.VMEM((NZ, 128, LANES), BF16),
        pltpu.VMEM((NZ, 128, LANES), F32),
        pltpu.VMEM((NX, 32, LANES), F32),
        pltpu.VMEM((NX, 32, LANES), BF16),
        pltpu.VMEM((NX, 32, LANES), BF16),
        pltpu.VMEM((NX, 32, LANES), F32),
        pltpu.VMEM((NX, 16, LANES), F32),
        pltpu.VMEM((NX, 16, LANES), F32),
        pltpu.VMEM((NZ, 8, LANES), F32),
        pltpu.VMEM((NZ, 8, LANES), F32),
        dma, dma, dma, dma((2,)),
        dma((2,)), dma((CH, 4)),
        dma((2,)), dma((2,)), dma((4,)),
        dma((6,)), dma((CH,)), dma((CH, 4)),
        dma, dma,
        dma, dma((CH,)),
        dma, dma((2, 2)), dma, dma((2,)),
        dma, dma, dma, dma,
    ]
    grad_hidden, grad_prob, grad_weight = pl.pallas_call(
        kernel,
        out_shape=(
            jax.ShapeDtypeStruct((pair, slots, units), BF16),
            jax.ShapeDtypeStruct((8, tok), F32),
            jax.ShapeDtypeStruct((256, pair * units), F32),
        ),
        in_specs=[anyspec, anyspec, anyspec, vm, vm, vm],
        out_specs=(anyspec, vm, anyspec),
        scratch_shapes=scratch,
        compiler_params=pltpu.CompilerParams(
            collective_id=0, has_side_effects=True, vmem_limit_bytes=67043328
        ),
        name="routed_backward",
    )(
        cotangent,
        hidden.reshape(pair, slots, units),
        down_weight,
        routes.T,
        gate_prob.T,
        sign_seed.reshape(16, 128),
    )
    return (
        grad_hidden.reshape(hidden.shape),
        grad_prob.T,
        grad_weight.reshape(256, pair, units),
    )


def solution(mesh):
    in_specs = (
        P(("dp", "expert"), None),
        P(("dp", "expert"), None),
        P(("dp", "expert"), None),
        P("dp", "expert", None, None, None),
        P("expert", None, None),
        P(),
    )
    out_specs = (
        P("dp", "expert", None, None, None),
        P(("dp", "expert"), None),
        P("dp", "expert", None),
    )
    return jax.shard_map(shards, mesh=mesh, in_specs=in_specs, out_specs=out_specs, check_vma=False)
```

time: 331 us -> 121 us (0.37)
  waiting for transfers between devices: 157 us -> 0 us
  Pallas kernels: 0 us -> 114 us
  local copies, waits for them, and re-layouts: 85.3 us -> 5.25 us
  matrix products: 35.2 us -> 0 us
  starting transfers between devices: 30.9 us -> 0 us
  between operations: 14.3 us -> 0.65 us
  other arithmetic: 8.27 us -> 0 us
    all_to_all x3 -> x0, waiting for transfers between devices: 147 us -> none  [the longest x1 139 us: shards(): lax.all_to_all(send_grad, 'expert', split_axis=1, concat_axis=1, tiled=True)]
    pallas_call x0 -> x1, Pallas kernels: none -> 114 us  [shards(): pl.pallas_call(kernel, out_shape=(jax.ShapeDtypeStruct((pair, slots, unit...]
    dot_general x3 -> x0, matrix products: 35.2 us -> none  [the longest x1 16.4 us: rotate(): jnp.einsum('ij,bjx->bix', hadamard(BLOCK), shaped, precision=lax.Precisio...]
    all_to_all x3 -> x0, starting transfers between devices: 30.7 us -> none  [the longest x1 11.9 us: shards(): lax.all_to_all(send_prob, 'expert', split_axis=1, concat_axis=1, tiled=True)]
    gather x9 -> x0, local copies, waits for them, and re-layouts: 30.2 us -> none  [the longest x1 9.46 us: shards(): jnp.take(gate_prob.reshape(-1), pair_table, axis=0, mode='fill', fill_val...]
    convert_element_type x4 -> x0, local copies, waits for them, and re-layouts: 29 us -> none  [the longest x2 28.8 us: shards(): rotate(product, sign_vec).astype(jnp.bfloat16)]
    unnamed x18 -> x6, local copies, waits for them, and re-layouts: 16.1 us -> 2.01 us
    reduce_scatter x1 -> x0, waiting for transfers between devices: 9.27 us -> none  [shards(): lax.psum_scatter(rotate(product, sign_vec).astype(jnp.bfloat16), 'dp', sc...]
  transfers between devices with their start and end apart: 4 -> 0, of which waited for: 3 -> 0; matrix products, arithmetic and copies ran while one was open for 10% -> 0% of each run, Pallas kernels for 0% -> 0%
where the time goes in v2:
time: 121 us; the launch traced here: 120 us
  Pallas kernels  114 us (94%)
  local copies, waits for them, and re-layouts  5.25 us (4%)
    pallas_call x1, Pallas kernels, shards(): pl.pallas_call(kernel, out_shape=(jax.ShapeDtypeStruct((pair, slots, unit...  114 us
    reshape x1, local copies, waits for them, and re-layouts, shards(): grad_weight.reshape(256, pair, units)  3.25 us

profile of v2, /device:TPU:1, one launch (start us, length us, event | category | flops | bytes accessed | tf_op | source)
XLA Modules:
  0.0 120.3 jit_solution(17682473791526529936)
XLA Ops:
  0.6 114.4 %routed_backward.1 = (bf16[2,768,768]{2,1,0:T(8,128)(2,1)}, f32[8,128]{1,0:T(8,128)}, f32[256,1536]{1,0:T(8,128)}) custom-call(bf16[128,2048]{1,0:T(8,128)(2,1)} %cot.1, bf16[2,768,768]{2,1,0:T(8,128)(2,1)} %bitcast.7, bf16[2,768,2048]{2,1,0:T(8,128)(2,1)} %w_hbm.1, s32[8,128]{1,0:T(8,128)} %bitcast.9, bf16[8,128]{1,0:T(8,128)(2,1)} %bitcast.11, ...), custom_call_target="tpu_custom_call" | custom-call | tf_op jit(solution)/shard_map/routed_backward/pallas_call | solution.py:530
  115.1 0.0 copy-start
  115.1 3.2 %reshape.21 = f32[256,2,768]{2,1,0:T(2,128)} reshape(f32[256,1536]{1,0:T(8,128)} %get-tuple-element.8) | data formatting | bytes 3145728 | tf_op jit(solution)/shard_map/reshape | solution.py:555
  118.3 0.0 copy-done
  118.3 0.0 copy-start.1
  118.3 1.4 %copy.11 = bf16[1,2,32,24,768]{4,3,2,1,0:T(8,128)(2,1)} copy(bf16[1,2,32,24,768]{4,3,2,1,0:T(8,128)(2,1)S(1)} %bitcast.6) | data formatting | bytes 4718592
  119.7 0.0 copy-done.1
  119.7 0.6 copy.12
Async XLA Ops:
  115.1 3.3 %copy-start = (bf16[2,768,768]{2,1,0:T(8,128)(2,1)S(1)}, bf16[2,768,768]{2,1,0:T(8,128)(2,1)}, u32[]{:S(2)}) copy-start(bf16[2,768,768]{2,1,0:T(8,128)(2,1)} %get-tuple-element.6) | copy-start | bytes 7077892
  118.3 1.4 %copy-start.1 = (f32[8,128]{1,0:T(8,128)S(1)}, f32[8,128]{1,0:T(8,128)}, u32[]{:S(2)}) copy-start(f32[8,128]{1,0:T(8,128)} %get-tuple-element.7) | copy-start | bytes 12292

commit v3 on v2

--- a/solution.py
+++ b/solution.py
@@ -192,9 +192,9 @@
     def step_of(s, t):
         if t < 0:
             s, t = s - 1, t + 8
-        tail = s == 3
+        tail = s >= 1
         return (
-            jnp.where(tail, 6 + t // 4, 2 * s + t % 2),
+            jnp.where(tail, 2 * s + t // 4, 2 * s + t % 2),
             jnp.where(tail, t % 4, t // 2),
         )
 
@@ -349,8 +349,8 @@
                     z_relay(2 * s + 2 + (t - 3) % 2, (t - 3) // 2)
 
             c, i = step_of(s, t)
-            if t in (3, 6, 7):
-                @pl.when(more & (i == 3))
+            if t in (3, 7):
+                @pl.when(more)
                 def _(c=c):
                     z_wait(c, 4)
             x_step(c, i)
@@ -362,66 +362,87 @@
             else:
                 x_forward(fc, fi)
 
-            a, b = 2 * s - 2, 2 * s - 1
+            at_one, later = s == 1, s > 1
+            if t == 0:
+                @pl.when(later)
+                def _():
+                    pair_add(2 * s - 3)
             if t == 2:
-                @pl.when(s == 1)
+                @pl.when(at_one)
                 def _():
                     weigh()
-            if t in (1, 2):
-                @pl.when(s > 1)
-                def _(t=t):
-                    finish(2 * s - 5 + t)
+
+                @pl.when(later)
+                def _():
+                    x_wait(2 * s - 2)
+                    partial(2 * s - 2)
+
+                @pl.when(s == 2)
+                def _():
+                    relay_add(0)
             if t == 3:
-                @pl.when(more)
-                def _():
-                    x_wait(a)
-                    partial(a)
+                @pl.when(later)
+                def _():
+                    back(2 * s - 2)
+                    relay_add(2 * s - 3)
             if t == 4:
-                @pl.when(more)
-                def _():
-                    x_wait(b)
-                    partial(b)
+                @pl.when(later)
+                def _():
+                    pair_add(2 * s - 2)
             if t == 5:
-                @pl.when(s == 1)
+                @pl.when(at_one)
                 def _():
                     pltpu.make_async_copy(wbuf, wbuf, w_sem).wait()
-
-                @pl.when(more)
-                def _():
-                    back(a)
-                    pair_add(a)
+                    x_wait(0)
+                    partial(0)
+                    back(0)
+
+                @pl.when(later)
+                def _():
+                    finish(jnp.where(s == 2, 0, 2))
             if t == 6:
                 @pl.when(more)
                 def _():
-                    back(b)
-                    pair_add(b)
+                    x_wait(2 * s - 1)
+                    partial(2 * s - 1)
             if t == 7:
                 @pl.when(first)
                 def _():
                     x_tables()
 
+                @pl.when(at_one)
+                def _():
+                    pair_add(0)
+
                 @pl.when(more)
                 def _():
-                    relay_add(a)
-                    relay_add(b)
+                    back(2 * s - 1)
+
+                @pl.when(later)
+                def _():
+                    relay_add(2 * s - 2)
+                    finish(2 * s - 3)
         return 0
 
     lax.fori_loop(0, CH // 2, double, 0)
 
     x_forward(7, 1)
     x_forward(7, 2)
+    pair_add(5)
     x_wait(6)
     partial(6)
     x_forward(7, 3)
     back(6)
     pair_add(6)
-    finish(4)
-    finish(5)
+    relay_add(5)
     x_wait(7)
     partial(7)
+    finish(4)
+    pair_add(7)
     back(7)
-    pair_add(7)
     relay_add(6)
+    finish(5)
+    relay_add(7)
 
     def outputs(p, _):
         at = pl.ds(pl.multiple_of(p * rows48, 16), rows48)
@@ -435,9 +456,7 @@
             r_tab[xs, pl.ds(row + 2 + j, 1), :] = jnp.sum(jnp.where(odd, slot, 0.0), axis=0, keepdims=True)
         return 0
 
-    lax.fori_loop(0, 8, outputs, 0)
-    relay_add(7)
-    lax.fori_loop(8, 16, outputs, 0)
+    lax.fori_loop(0, 16, outputs, 0)
 
     for d in range(1, NX):
         to = up(x, d, NX)

time: 121 us -> 115 us (0.950)
  Pallas kernels: 114 us -> 108 us
    pallas_call x1, Pallas kernels: 114 us -> 108 us  [shards(): pl.pallas_call(kernel, out_shape=(jax.ShapeDtypeStruct((pair, slots, unit...]
where the time goes in v3:
time: 115 us; the launch traced here: 114 us
  Pallas kernels  108 us (94%)
  local copies, waits for them, and re-layouts  5.25 us (5%)
    pallas_call x1, Pallas kernels, shards(): pl.pallas_call(kernel, out_shape=(jax.ShapeDtypeStruct((pair, slots, unit...  108 us
    reshape x1, local copies, waits for them, and re-layouts, shards(): grad_weight.reshape(256, pair, units)  3.25 us

profile of v3, /device:TPU:1, one launch (start us, length us, event | category | flops | bytes accessed | tf_op | source)
XLA Modules:
  0.0 114.4 jit_solution(14332276885408834746)
XLA Ops:
  0.6 108.5 %routed_backward.1 = (bf16[2,768,768]{2,1,0:T(8,128)(2,1)}, f32[8,128]{1,0:T(8,128)}, f32[256,1536]{1,0:T(8,128)}) custom-call(bf16[128,2048]{1,0:T(8,128)(2,1)} %cot.1, bf16[2,768,768]{2,1,0:T(8,128)(2,1)} %bitcast.7, bf16[2,768,2048]{2,1,0:T(8,128)(2,1)} %w_hbm.1, s32[8,128]{1,0:T(8,128)} %bitcast.9, bf16[8,128]{1,0:T(8,128)(2,1)} %bitcast.11, ...), custom_call_target="tpu_custom_call" | custom-call | tf_op jit(solution)/shard_map/routed_backward/pallas_call | solution.py:549
  109.1 0.0 copy-start
  109.1 3.2 %reshape.21 = f32[256,2,768]{2,1,0:T(2,128)} reshape(f32[256,1536]{1,0:T(8,128)} %get-tuple-element.8) | data formatting | bytes 3145728 | tf_op jit(solution)/shard_map/reshape | solution.py:574
  112.4 0.0 copy-done
  112.4 0.0 copy-start.1
  112.4 1.4 %copy.11 = bf16[1,2,32,24,768]{4,3,2,1,0:T(8,128)(2,1)} copy(bf16[1,2,32,24,768]{4,3,2,1,0:T(8,128)(2,1)S(1)} %bitcast.6) | data formatting | bytes 4718592
  113.8 0.0 copy-done.1
  113.8 0.6 copy.12
Async XLA Ops:
  109.1 3.3 %copy-start = (bf16[2,768,768]{2,1,0:T(8,128)(2,1)S(1)}, bf16[2,768,768]{2,1,0:T(8,128)(2,1)}, u32[]{:S(2)}) copy-start(bf16[2,768,768]{2,1,0:T(8,128)(2,1)} %get-tuple-element.6) | copy-start | bytes 7077892
  112.4 1.4 %copy-start.1 = (f32[8,128]{1,0:T(8,128)S(1)}, f32[8,128]{1,0:T(8,128)}, u32[]{:S(2)}) copy-start(f32[8,128]{1,0:T(8,128)} %get-tuple-element.7) | copy-start | bytes 12292

commit v4 on v3

--- a/solution.py
+++ b/solution.py
@@ -437,12 +437,9 @@
     relay_add(5)
     x_wait(7)
     partial(7)
-    finish(4)
+    back(7)
     pair_add(7)
-    back(7)
     relay_add(6)
-    finish(5)
-    relay_add(7)
 
     def outputs(p, _):
         at = pl.ds(pl.multiple_of(p * rows48, 16), rows48)
@@ -456,14 +453,17 @@
             r_tab[xs, pl.ds(row + 2 + j, 1), :] = jnp.sum(jnp.where(odd, slot, 0.0), axis=0, keepdims=True)
         return 0
 
-    lax.fori_loop(0, 16, outputs, 0)
+    lax.fori_loop(0, 8, outputs, 0)
+    relay_add(7)
+    lax.fori_loop(8, 16, outputs, 0)
 
     for d in range(1, NX):
         to = up(x, d, NX)
         remote(r_tab.at[to], r_mid.at[x], rx_send, rx_recv, x_dev(to)).start()
     r_mid[x] = r_tab[x]
     pltpu.make_async_copy(gh_buf, gh_out, hid_sem).start()
-    finish(6)
+    finish(4)
+    finish(5)
     wait_recv(r_mid.at[pl.ds(0, 3)], rx_recv)
     for zs in range(NZ):
         for xx in range(NX):
@@ -472,6 +472,7 @@
         to = up(z, d, NZ)
         remote(r_out.at[to], r_end.at[z], rz_send, rz_recv, z_dev(to)).start()
     r_end[z] = r_out[z]
+    finish(6)
     finish(7)
     wait_recv(r_end.at[pl.ds(0, 7)], rz_recv)
     grad_prob = jnp.zeros((8, LANES), F32)

time: 115 us -> 113 us (0.983)
    pallas_call x1, Pallas kernels: 108 us -> 107 us  [shards(): pl.pallas_call(kernel, out_shape=(jax.ShapeDtypeStruct((pair, slots, unit...]
where the time goes in v4:
time: 113 us
  Pallas kernels  107 us (95%)
  local copies, waits for them, and re-layouts  5.25 us (5%)
    pallas_call x1, Pallas kernels, shards(): pl.pallas_call(kernel, out_shape=(jax.ShapeDtypeStruct((pair, slots, unit...  107 us
    reshape x1, local copies, waits for them, and re-layouts, shards(): grad_weight.reshape(256, pair, units)  3.25 us

profile of v4, /device:TPU:1, one launch (start us, length us, event | category | flops | bytes accessed | tf_op | source)
XLA Modules:
  0.0 112.6 jit_solution(17478834427987890988)
XLA Ops:
  0.6 106.7 %routed_backward.1 = (bf16[2,768,768]{2,1,0:T(8,128)(2,1)}, f32[8,128]{1,0:T(8,128)}, f32[256,1536]{1,0:T(8,128)}) custom-call(bf16[128,2048]{1,0:T(8,128)(2,1)} %cot.1, bf16[2,768,768]{2,1,0:T(8,128)(2,1)} %bitcast.7, bf16[2,768,2048]{2,1,0:T(8,128)(2,1)} %w_hbm.1, s32[8,128]{1,0:T(8,128)} %bitcast.9, bf16[8,128]{1,0:T(8,128)(2,1)} %bitcast.11, ...), custom_call_target="tpu_custom_call" | custom-call | tf_op jit(solution)/shard_map/routed_backward/pallas_call | solution.py:550
  107.4 0.0 copy-start
  107.4 3.2 %reshape.21 = f32[256,2,768]{2,1,0:T(2,128)} reshape(f32[256,1536]{1,0:T(8,128)} %get-tuple-element.8) | data formatting | bytes 3145728 | tf_op jit(solution)/shard_map/reshape | solution.py:575
  110.6 0.0 copy-done
  110.6 0.0 copy-start.1
  110.6 1.4 %copy.11 = bf16[1,2,32,24,768]{4,3,2,1,0:T(8,128)(2,1)} copy(bf16[1,2,32,24,768]{4,3,2,1,0:T(8,128)(2,1)S(1)} %bitcast.6) | data formatting | bytes 4718592
  112.0 0.0 copy-done.1
  112.0 0.6 copy.12
Async XLA Ops:
  107.4 3.3 %copy-start = (bf16[2,768,768]{2,1,0:T(8,128)(2,1)S(1)}, bf16[2,768,768]{2,1,0:T(8,128)(2,1)}, u32[]{:S(2)}) copy-start(bf16[2,768,768]{2,1,0:T(8,128)(2,1)} %get-tuple-element.6) | copy-start | bytes 7077892
  110.6 1.4 %copy-start.1 = (f32[8,128]{1,0:T(8,128)S(1)}, f32[8,128]{1,0:T(8,128)}, u32[]{:S(2)}) copy-start(f32[8,128]{1,0:T(8,128)} %get-tuple-element.7) | copy-start | bytes 12292

commit v5 on v4

--- a/solution.py
+++ b/solution.py
@@ -433,10 +433,10 @@
     partial(6)
     x_forward(7, 3)
     back(6)
+    x_wait(7)
+    partial(7)
     pair_add(6)
     relay_add(5)
-    x_wait(7)
-    partial(7)
     back(7)
     pair_add(7)
     relay_add(6)

time: 113 us -> 114 us (level)
  no operation moved by 1% of the time
where the time goes in v5:
time: 114 us; the launch traced here: 113 us
  Pallas kernels  107 us (94%)
  local copies, waits for them, and re-layouts  5.25 us (5%)
    pallas_call x1, Pallas kernels, shards(): pl.pallas_call(kernel, out_shape=(jax.ShapeDtypeStruct((pair, slots, unit...  107 us
    reshape x1, local copies, waits for them, and re-layouts, shards(): grad_weight.reshape(256, pair, units)  3.25 us

profile of v5, /device:TPU:1, one launch (start us, length us, event | category | flops | bytes accessed | tf_op | source)
XLA Modules:
  0.0 112.6 jit_solution(12369070436717261937)
XLA Ops:
  0.6 106.7 %routed_backward.1 = (bf16[2,768,768]{2,1,0:T(8,128)(2,1)}, f32[8,128]{1,0:T(8,128)}, f32[256,1536]{1,0:T(8,128)}) custom-call(bf16[128,2048]{1,0:T(8,128)(2,1)} %cot.1, bf16[2,768,768]{2,1,0:T(8,128)(2,1)} %bitcast.7, bf16[2,768,2048]{2,1,0:T(8,128)(2,1)} %w_hbm.1, s32[8,128]{1,0:T(8,128)} %bitcast.9, bf16[8,128]{1,0:T(8,128)(2,1)} %bitcast.11, ...), custom_call_target="tpu_custom_call" | custom-call | tf_op jit(solution)/shard_map/routed_backward/pallas_call | solution.py:550
  107.4 0.0 copy-start
  107.4 3.2 %reshape.21 = f32[256,2,768]{2,1,0:T(2,128)} reshape(f32[256,1536]{1,0:T(8,128)} %get-tuple-element.8) | data formatting | bytes 3145728 | tf_op jit(solution)/shard_map/reshape | solution.py:575
  110.6 0.0 copy-done
  110.6 0.0 copy-start.1
  110.6 1.4 %copy.11 = bf16[1,2,32,24,768]{4,3,2,1,0:T(8,128)(2,1)} copy(bf16[1,2,32,24,768]{4,3,2,1,0:T(8,128)(2,1)S(1)} %bitcast.6) | data formatting | bytes 4718592
  112.0 0.0 copy-done.1
  112.0 0.6 copy.12
Async XLA Ops:
  107.4 3.3 %copy-start = (bf16[2,768,768]{2,1,0:T(8,128)(2,1)S(1)}, bf16[2,768,768]{2,1,0:T(8,128)(2,1)}, u32[]{:S(2)}) copy-start(bf16[2,768,768]{2,1,0:T(8,128)(2,1)} %get-tuple-element.6) | copy-start | bytes 7077892
  110.6 1.4 %copy-start.1 = (f32[8,128]{1,0:T(8,128)S(1)}, f32[8,128]{1,0:T(8,128)}, u32[]{:S(2)}) copy-start(f32[8,128]{1,0:T(8,128)} %get-tuple-element.7) | copy-start | bytes 12292

commit v6 on v4

--- a/solution.py
+++ b/solution.py
@@ -453,13 +453,13 @@
             r_tab[xs, pl.ds(row + 2 + j, 1), :] = jnp.sum(jnp.where(odd, slot, 0.0), axis=0, keepdims=True)
         return 0
 
-    lax.fori_loop(0, 8, outputs, 0)
-    relay_add(7)
-    lax.fori_loop(8, 16, outputs, 0)
-
-    for d in range(1, NX):
+    for d in (2, 1, 3, 0):
         to = up(x, d, NX)
-        remote(r_tab.at[to], r_mid.at[x], rx_send, rx_recv, x_dev(to)).start()
+        lax.fori_loop(0, 4, lambda m, t, to=to: outputs(4 * to + m, t), 0)
+        if d > 0:
+            remote(r_tab.at[to], r_mid.at[x], rx_send, rx_recv, x_dev(to)).start()
+        if d == 1:
+            relay_add(7)
     r_mid[x] = r_tab[x]
     pltpu.make_async_copy(gh_buf, gh_out, hid_sem).start()
     finish(4)

time: 113 us -> 113 us (level); the launches traced: 113 us -> 111 us
  Pallas kernels: 107 us -> 105 us
    pallas_call x1, Pallas kernels: 107 us -> 105 us  [shards(): pl.pallas_call(kernel, out_shape=(jax.ShapeDtypeStruct((pair, slots, unit...]
where the time goes in v6:
time: 113 us; the launch traced here: 111 us
  Pallas kernels  105 us (93%)
  local copies, waits for them, and re-layouts  5.25 us (5%)
    pallas_call x1, Pallas kernels, shards(): pl.pallas_call(kernel, out_shape=(jax.ShapeDtypeStruct((pair, slots, unit...  105 us
    reshape x1, local copies, waits for them, and re-layouts, shards(): grad_weight.reshape(256, pair, units)  3.25 us

profile of v6, /device:TPU:1, one launch (start us, length us, event | category | flops | bytes accessed | tf_op | source)
XLA Modules:
  0.0 110.8 jit_solution(7739406825807796570)
XLA Ops:
  0.6 104.9 %routed_backward.1 = (bf16[2,768,768]{2,1,0:T(8,128)(2,1)}, f32[8,128]{1,0:T(8,128)}, f32[256,1536]{1,0:T(8,128)}) custom-call(bf16[128,2048]{1,0:T(8,128)(2,1)} %cot.1, bf16[2,768,768]{2,1,0:T(8,128)(2,1)} %bitcast.7, bf16[2,768,2048]{2,1,0:T(8,128)(2,1)} %w_hbm.1, s32[8,128]{1,0:T(8,128)} %bitcast.9, bf16[8,128]{1,0:T(8,128)(2,1)} %bitcast.11, ...), custom_call_target="tpu_custom_call" | custom-call | tf_op jit(solution)/shard_map/routed_backward/pallas_call | solution.py:550
  105.6 0.0 copy-start
  105.6 3.2 %reshape.21 = f32[256,2,768]{2,1,0:T(2,128)} reshape(f32[256,1536]{1,0:T(8,128)} %get-tuple-element.8) | data formatting | bytes 3145728 | tf_op jit(solution)/shard_map/reshape | solution.py:575
  108.8 0.0 copy-done
  108.8 0.0 copy-start.1
  108.8 1.4 %copy.11 = bf16[1,2,32,24,768]{4,3,2,1,0:T(8,128)(2,1)} copy(bf16[1,2,32,24,768]{4,3,2,1,0:T(8,128)(2,1)S(1)} %bitcast.6) | data formatting | bytes 4718592
  110.2 0.0 copy-done.1
  110.2 0.6 copy.12
Async XLA Ops:
  105.6 3.3 %copy-start = (bf16[2,768,768]{2,1,0:T(8,128)(2,1)S(1)}, bf16[2,768,768]{2,1,0:T(8,128)(2,1)}, u32[]{:S(2)}) copy-start(bf16[2,768,768]{2,1,0:T(8,128)(2,1)} %get-tuple-element.6) | copy-start | bytes 7077892
  108.8 1.4 %copy-start.1 = (f32[8,128]{1,0:T(8,128)S(1)}, f32[8,128]{1,0:T(8,128)}, u32[]{:S(2)}) copy-start(f32[8,128]{1,0:T(8,128)} %get-tuple-element.7) | copy-start | bytes 12292
